TPU v7x, 1024 devices: a whole 4x4x32 slice. The times are simulated.
1024 devices in a mesh: fsdp: 64 (over y_hi, z), seq: 16 (over y_lo, x, core).
Axes of the slice: x: 4, y: 4 (y_hi: 2, y_lo: 2; y = y_hi * 2 + y_lo), z: 32, core: 2. Of those that a mesh axis runs over, the one named last changes fastest.
Arguments:
- clips_in: bfloat16 [64, 16, 384, 320], P('fsdp', 'seq'), may hold values from -81 to 81
- weight_space: bfloat16 [320, 2880], P('fsdp'), may hold values from -0.109375 to 0.109375
- weight_time: bfloat16 [320, 960], P('fsdp'), may hold values from -0.1875 to 0.1875
- norm_gain: float32 [320], replicated, may hold values from 0.1 to 1.9
- norm_shift: float32 [320], replicated, may hold values from -2 to 2
- out_grad: bfloat16 [64, 16, 384, 320], P('fsdp', 'seq'), may hold values from -16 to 16
Outputs:
- mixed: bfloat16 [64, 16, 384, 320], P('fsdp', 'seq')
- in_grad: bfloat16 [64, 16, 384, 320], P('fsdp', 'seq')
- grad_time: float32 [320, 960], P('fsdp')
All inputs are finite; a program needn't handle non-finite values.
Results may differ from a plain program's by a relative error of at most 0.015.
Values may be sent and summed in bfloat16 or wider, within the bound.
A program may use at most 32 MiB of HBM per device.

v0:
```python
import jax
import jax.numpy as jnp
from jax import lax
from jax.sharding import PartitionSpec as P

GROUPS = 32
FRAMES = 16
HEIGHT = 16
WIDTH = 24


EPSILON = 1e-05


def extended_2(value, sides, width):
    for axis, dim in sides:
        size, length = (lax.axis_size(axis), value.shape[dim])
        up = [(i, (i + 1) % size) for i in range(size - 1)]
        down = [(j, i) for i, j in up]
        last = lax.slice_in_dim(value, length - width, length, axis=dim)
        leading = lax.slice_in_dim(value, 0, width, axis=dim)
        before = lax.ppermute(last, axis, up)
        after = lax.ppermute(leading, axis, down)
        value = jnp.concatenate([before, value, after], axis=dim)
    return value


def contract_last(left_rows, right_rows):
    return lax.dot_general(
        left_rows, right_rows, (((1,), (1,)), ((), ())), preferred_element_type=jnp.float32
    )


def contract_first(left_rows, right_rows):
    return lax.dot_general(
        left_rows, right_rows, (((0,), (0,)), ((), ())), preferred_element_type=jnp.float32
    )


def padded_grid(flat_values, frame_count):
    channels = flat_values.shape[-1]
    image_grid = flat_values.reshape(frame_count, HEIGHT, WIDTH, channels)
    return jnp.pad(image_grid, ((0, 0), (1, 1), (1, 1), (0, 0)))


def grid_window(padded, offset):
    shift_row, shift_col = (offset // 3, offset % 3)
    frame_count = padded.shape[0]
    channels = padded.shape[-1]
    window = padded[:, shift_row : shift_row + HEIGHT, shift_col : shift_col + WIDTH, :]
    return window.reshape(frame_count * HEIGHT * WIDTH, channels)


def conv_space(frames_in, weight):
    padded = padded_grid(frames_in, frames_in.shape[0])
    stacked = jnp.concatenate([grid_window(padded, offset) for offset in range(9)], axis=1)
    return contract_last(stacked, weight)


def conv_space_back(grad_rows, weight, frame_count):
    channels = weight.shape[0]
    padded = padded_grid(grad_rows, frame_count)
    stacked = jnp.concatenate([grid_window(padded, 8 - offset) for offset in range(9)], axis=1)
    flipped = (
        weight.reshape(channels, 9, channels).transpose(1, 0, 2).reshape(9 * channels, channels)
    )
    return jnp.dot(stacked, flipped, preferred_element_type=jnp.float32)


def conv_time(extended, weight):
    clip_count, frames_ext, pixels, channels = extended.shape
    frame_count = frames_ext - 2
    summed = jnp.zeros((clip_count * frame_count * pixels, channels), jnp.float32)
    for offset in range(3):
        slab_rows = extended[:, offset : offset + frame_count].reshape(-1, channels)
        summed = summed + contract_last(
            slab_rows, weight[:, offset * channels : (offset + 1) * channels]
        )
    return summed.reshape(clip_count, frame_count, pixels, channels)


def conv_time_back(extended, weight):
    clip_count, frames_ext, pixels, channels = extended.shape
    frame_count = frames_ext - 2
    summed = jnp.zeros((clip_count * frame_count * pixels, channels), jnp.float32)
    for offset in range(3):
        slab_rows = extended[:, 2 - offset : 2 - offset + frame_count].reshape(-1, channels)
        summed = summed + jnp.dot(
            slab_rows,
            weight[:, offset * channels : (offset + 1) * channels],
            preferred_element_type=jnp.float32,
        )
    return summed.reshape(clip_count, frame_count, pixels, channels)


def group_mean(totals, counted):
    clip_count, channels = totals.shape
    per_group = channels // GROUPS
    average = totals.reshape(clip_count, GROUPS, per_group).sum(-1) / counted
    return jnp.repeat(average, per_group, axis=1)


def group_totals(first_sums, second_sums):
    return lax.psum((first_sums, second_sums), "seq")


def frame_rims(values):
    return extended_2(values, (("seq", 1),), 1)


def local(clips_in, weight_space, weight_time, norm_gain, norm_shift, out_grad):
    full_space, full_time = (
        lax.all_gather(weight_space, "fsdp", axis=0, tiled=True),
        lax.all_gather(weight_time, "fsdp", axis=0, tiled=True),
    )
    clip_count, frame_dev, pixels, channels = clips_in.shape
    counted = FRAMES * pixels * (channels // GROUPS)
    frames_in = clips_in.reshape(clip_count * frame_dev, pixels, channels)
    hidden = conv_space(frames_in, full_space).reshape(clip_count, frame_dev, pixels, channels)
    first_sums, second_sums = group_totals(
        jnp.sum(hidden, axis=(1, 2)), jnp.sum(hidden * hidden, axis=(1, 2))
    )
    average = group_mean(first_sums, counted)
    squares = group_mean(second_sums, counted)
    inv_std = lax.rsqrt(squares - average * average + EPSILON)
    normed = (hidden - average[:, None, None, :]) * inv_std[:, None, None, :]
    preact = normed * norm_gain + norm_shift
    activation = jax.nn.silu(preact).astype(jnp.bfloat16)
    act_ext = frame_rims(activation)
    grad_ext = frame_rims(out_grad)
    mixed = conv_time(act_ext, full_time).astype(jnp.bfloat16)
    act_grad = conv_time_back(grad_ext, full_time).astype(jnp.bfloat16)
    sigmoid_val = jax.nn.sigmoid(preact)
    slopes = sigmoid_val * (1.0 + preact * (1.0 - sigmoid_val))
    scaled = act_grad.astype(jnp.float32) * slopes * norm_gain
    first_back, second_back = group_totals(
        jnp.sum(scaled, axis=(1, 2)), jnp.sum(scaled * normed, axis=(1, 2))
    )
    mean_one = group_mean(first_back, counted)
    mean_two = group_mean(second_back, counted)
    hid_grad = (
        inv_std[:, None, None, :]
        * (scaled - mean_one[:, None, None, :] - normed * mean_two[:, None, None, :])
    ).astype(jnp.bfloat16)
    grad_rows = hid_grad.reshape(-1, channels)
    in_grad = (
        conv_space_back(grad_rows, full_space, clip_count * frame_dev)
        .reshape(clips_in.shape)
        .astype(jnp.bfloat16)
    )
    time_rows = out_grad.reshape(-1, channels)
    time_frames = out_grad.shape[1]
    time_stack = jnp.concatenate(
        [act_ext[:, offset : offset + time_frames].reshape(-1, channels) for offset in range(3)],
        axis=1,
    )
    time_part = lax.psum_scatter(
        contract_first(time_rows, time_stack), "fsdp", scatter_dimension=0, tiled=True
    )
    time_sum = lax.psum(time_part, "seq")
    factor = 1.0 / (lax.axis_size("fsdp") * clip_count * FRAMES)
    return (mixed, in_grad, time_sum * factor)


def solution(mesh):
    in_specs = (
        P("fsdp", "seq", None, None),
        P("fsdp", None),
        P("fsdp", None),
        P(),
        P(),
        P("fsdp", "seq", None, None),
    )
    out_specs = (P("fsdp", "seq", None, None), P("fsdp", "seq", None, None), P("fsdp", None))
    return jax.shard_map(local, mesh=mesh, in_specs=in_specs, out_specs=out_specs, check_vma=False)
```

profile of v0, /device:TPU:1, one launch (start us, length us, event | category | flops | bytes accessed | tf_op | source)
XLA Modules:
  0.0 1036.6 jit_solution(4712828854720901101)
XLA Ops:
  7.2 0.7 all-gather.4.cloned.1.call-update
  8.0 4.5 collective-permute-start.3
  12.5 13.5 %collective-permute-start.2 = (bf16[1,1,384,320]{2,3,1,0:T(8,128)(2,1)}, bf16[1,1,384,320]{2,3,1,0:T(8,128)(2,1)}, u32[]{:S(2)}, u32[]{:S(2)}) collective-permute-start(bf16[1,1,384,320]{2,3,1,0:T(8,128)(2,1)} %param.11), channel_id=1, source_target_pairs={{1,0},{2,1},{3,2},{4,3},{5,4},{6,5},{7,6},{8,7},{9,8},{10,9},{11,1... | collective-permute-start | bytes 737288 | tf_op jit(solution)/shard_map/ppermute | solution.py:23
  26.0 126.7 %all-gather.1 = bf16[64,5,960]{2,1,0:T(8,128)(2,1)S(1)} all-gather(bf16[1,5,960]{2,1,0:T(8,128)(2,1)} %bitcast.81), channel_id=1, replica_groups=mesh['fsdp'=64,'seq'=16] {'fsdp'}, dimensions={0}, use_global_device_ids=true | all-gather | bytes 624000 | tf_op jit(solution)/shard_map/all_gather | solution.py:114
  152.7 0.4 reshape.246
  153.4 1.4 pad_slice_fusion.8
  154.9 3.9 concatenate.9
  158.7 2.3 fusion.17
  161.0 2.1 fusion.14
  163.1 123.1 %all-gather.4.cloned.1.call-done = bf16[64,5,2880]{2,1,0:T(8,128)(2,1)} async-done(((bf16[1,5,2880]{2,1,0:T(8,128)(2,1)}), bf16[64,5,2880]{2,1,0:T(8,128)(2,1)}) %all-gather.4.cloned.1.call-update) | async-done | bytes 1843216 | tf_op jit(solution)/shard_map/all_gather | solution.py:113
  286.1 4.5 reshape.244
  290.7 2.8 fusion.32
  293.7 67.8 %all-reduce.4 = (f32[32,10]{1,0:T(8,128)S(1)}, f32[32,10]{1,0:T(8,128)S(1)}) all-reduce(f32[32,10]{1,0:T(8,128)S(1)} %reshape.221, f32[32,10]{1,0:T(8,128)S(1)} %reshape.220), channel_id=1, replica_groups=mesh['fsdp'=64,'seq'=16] {'seq'}, use_global_device_ids=true, to_apply=%region_4.5 | all-reduce | flops 640 | bytes 5120 | tf_op jit(solution)/shard_map/psum | solution.py:104
  362.2 2.0 fusion.31
  364.3 6.6 collective-permute-start.1
  370.9 1.9 collective-permute-start
  372.9 3.1 collective-permute-done
  376.0 0.7 copy-done.6
  376.6 1.6 convolution_bitcast_fusion
  378.3 1.3 dynamic-slice
  380.4 3.8 reshape.237
  384.2 2.7 copy.32
  387.0 0.4 fusion.24
  387.4 0.3 fusion.21
  387.7 1.0 fusion.8
  388.7 516.9 %all-reduce.7.cloned.1.call-done = f32[320,960]{1,0:T(8,128)} async-done(((f32[320,960]{1,0:T(8,128)}), f32[320,960]{1,0:T(8,128)}) %all-reduce.7.cloned.1.call-update) | async-done | bytes 1228816
  905.6 0.8 constant_dynamic-slice_fusion
  906.4 91.3 %all-reduce.3 = (f32[32,10]{1,0:T(8,128)S(1)}, f32[32,10]{1,0:T(8,128)S(1)}, f32[5,960]{1,0:T(8,128)}) all-reduce(f32[32,10]{1,0:T(8,128)S(1)} %reshape.228, f32[32,10]{1,0:T(8,128)S(1)} %reshape.227, f32[5,960]{1,0:T(8,128)S(1)} %constant_dynamic-slice_fusion), channel_id=1, replica_groups=mesh['fsdp'=64,'seq'=16] {'seq'}, use_global_device_ids=true, to_apply=%region_10.11 | all-reduce | flops 5440 | bytes 43520 | tf_op jit(solution)/shard_map/psum | solution.py:104
  998.4 0.2 multiply_convert_fusion
  998.6 0.9 copy.23
  999.5 3.7 pad_slice_fusion
  1003.2 1.8 copy.24
  1005.0 1.6 constant_dynamic-update-slice_fusion.8
  1006.7 1.8 copy.25
  1008.5 1.8 copy.26
  1010.3 1.8 copy.27
  1012.1 1.7 constant_dynamic-update-slice_fusion.7
  1013.8 1.7 constant_dynamic-update-slice_fusion.6
  1015.4 1.7 constant_dynamic-update-slice_fusion.5
  1017.1 0.7 constant_dynamic-update-slice_fusion.4
  1017.8 1.8 copy.28
  1019.6 0.8 copy.29
  1020.9 0.6 broadcast_multiply_fusion
  1021.5 1.7 constant_dynamic-update-slice_fusion.3
  1023.2 1.7 constant_dynamic-update-slice_fusion.2
  1024.8 0.7 constant_dynamic-update-slice_fusion.1
  1025.5 0.7 constant_dynamic-update-slice_fusion
  1026.3 3.5 fusion.7
  (61 shorter events, 2.4 us)
Async XLA Ops:
  7.2 146.0 %copy-start.5 = (bf16[1,1,384,320]{2,3,1,0:T(8,128)(2,1)S(1)}, bf16[1,1,384,320]{2,3,1,0:T(8,128)(2,1)}, u32[]{:S(2)}) copy-start(bf16[1,1,384,320]{2,3,1,0:T(8,128)(2,1)} %param.6) | copy-start | bytes 737284
  7.2 279.0 %all-gather.4.cloned.1.call-start = ((), (), s32[]{:S(2)}) async-start(), calls=%async_computation | async-start | bytes 3061760 | tf_op jit(solution)/shard_map/all_gather | solution.py:113
  7.9 897.7 %all-reduce.7.cloned.1.call-start = ((), (), s32[]{:S(2)}) async-start(), calls=%async_computation.1 | async-start | bytes 2621440
  8.0 153.0 %collective-permute-start.3 = (bf16[1,1,384,320]{2,3,1,0:T(8,128)(2,1)}, bf16[1,1,384,320]{2,3,1,0:T(8,128)(2,1)}, u32[]{:S(2)}, u32[]{:S(2)}) collective-permute-start(bf16[1,1,384,320]{2,3,1,0:T(8,128)(2,1)} %param.11), channel_id=1, source_target_pairs={{0,1},{1,2},{2,3},{3,4},{4,5},{5,6},{6,7},{7,8},{8,9},{9,10},{10,1... | collective-permute-start | bytes 737288 | tf_op jit(solution)/shard_map/ppermute | solution.py:22
  12.5 349.7 %collective-permute-start.2 = (bf16[1,1,384,320]{2,3,1,0:T(8,128)(2,1)}, bf16[1,1,384,320]{2,3,1,0:T(8,128)(2,1)}, u32[]{:S(2)}, u32[]{:S(2)}) collective-permute-start(bf16[1,1,384,320]{2,3,1,0:T(8,128)(2,1)} %param.11), channel_id=1, source_target_pairs={{1,0},{2,1},{3,2},{4,3},{5,4},{6,5},{7,6},{8,7},{9,8},{10,9},{11,1... | collective-permute-start | bytes 737288 | tf_op jit(solution)/shard_map/ppermute | solution.py:23
  153.2 209.0 %copy-start.1 = (bf16[320,960]{1,0:T(8,128)(2,1)}, bf16[320,960]{1,0:T(8,128)(2,1)S(1)}, u32[]{:S(2)}) copy-start(bf16[320,960]{1,0:T(8,128)(2,1)S(1)} %reshape.246) | copy-start | bytes 1843204
  290.7 71.5 %copy-start.14 = (f32[320]{0:T(512)S(1)}, f32[320]{0:T(512)}, u32[]{:S(2)}) copy-start(f32[320]{0:T(512)} %param.10) | copy-start | bytes 3844
  290.7 71.6 %copy-start.15 = (f32[320]{0:T(512)S(1)}, f32[320]{0:T(512)}, u32[]{:S(2)}) copy-start(f32[320]{0:T(512)} %param.9) | copy-start | bytes 3844
  293.5 68.7 %copy-start.3 = (f32[384,320]{0,1:T(8,128)}, f32[384,320]{0,1:T(8,128)S(1)}, u32[]{:S(2)}) copy-start(f32[384,320]{0,1:T(8,128)S(1)} %get-tuple-element.29) | copy-start | bytes 1474564
  362.2 14.4 %copy-start.8 = (bf16[1,1,384,320]{2,3,1,0:T(8,128)(2,1)S(1)}, bf16[1,1,384,320]{2,3,1,0:T(8,128)(2,1)}, u32[]{:S(2)}) copy-start(bf16[1,1,384,320]{2,3,1,0:T(8,128)(2,1)} %param.11) | copy-start | bytes 737284
  364.3 11.7 %copy-start.9 = (bf16[384,320]{0,1:T(8,128)(2,1)}, bf16[384,320]{0,1:T(8,128)(2,1)S(1)}, u32[]{:S(2)}) copy-start(bf16[384,320]{0,1:T(8,128)(2,1)S(1)} %get-tuple-element.12) | copy-start | bytes 737284
  364.3 16.2 %copy-start = (bf16[64,5,2880]{2,1,0:T(8,128)(2,1)S(1)}, bf16[64,5,2880]{2,1,0:T(8,128)(2,1)}, u32[]{:S(2)}) copy-start(bf16[64,5,2880]{2,1,0:T(8,128)(2,1)} %all-gather.4.cloned.1.call-done) | copy-start | bytes 5529604
  364.3 8.6 collective-permute-start.1
  370.9 5.0 collective-permute-start
  372.8 3.1 copy-start.11
  376.0 0.7 copy-start.6
  384.2 2.8 copy-start.2
  384.2 2.8 copy-start.10
  384.2 3.1 copy-start.12
  384.2 3.5 copy-start.7
  387.0 611.4 %copy-start.4 = (f32[384,320]{0,1:T(8,128)S(1)}, f32[384,320]{0,1:T(8,128)}, u32[]{:S(2)}) copy-start(f32[384,320]{0,1:T(8,128)} %copy-done.3) | copy-start | bytes 1474564
  1010.3 10.6 %copy-start.13 = (f32[5,960]{1,0:T(8,128)S(1)}, f32[5,960]{1,0:T(8,128)}, u32[]{:S(2)}) copy-start(f32[5,960]{1,0:T(8,128)} %get-tuple-element.9) | copy-start | bytes 57604
Sparse Core Ops, SparseCore 0:
  12.3 273.8 all-gather.3
  378.4 527.1 all-reduce.6
where the time goes:
time: 1040 us
  waiting for transfers between devices  644 us (62%)
  blocking collectives  286 us (28%)
  local copies, waits for them, and re-layouts  48 us (5%)
  starting transfers between devices  26.6 us (3%)
  matrix products  16 us (2%)
  between operations  15 us (1%)
    unnamed x3, waiting for transfers between devices  518 us
    psum x2, blocking collectives, group_totals(): return lax.psum((first_sums, second_sums), 'seq')  159 us
    all_gather x1, blocking collectives, local(): lax.all_gather(weight_time, 'fsdp', axis=0, tiled=True)  127 us
    all_gather x1, waiting for transfers between devices, local(): lax.all_gather(weight_space, 'fsdp', axis=0, tiled=True)  123 us
  transfers between devices with their start and end apart: 6, of which 3 were waited for; matrix products, arithmetic and copies ran while one was open for 3% of the time, Pallas kernels for 0%

commit v1 on v0

v1 whole, which is shorter than its diff:
```python
import jax
import jax.numpy as jnp
from jax import lax
from jax.experimental import pallas as pl
from jax.experimental.pallas import tpu as pltpu
from jax.sharding import PartitionSpec as P

GROUPS = 32
FRAMES = 16
HEIGHT = 16
WIDTH = 24
PIXELS = HEIGHT * WIDTH
CH = 320
EPSILON = 1e-05
NZ = 32
NEAR = (-3, -2, -1, 1, 2, 3, 4)
TIME_AT = 3072
COLS = 4096
BLK = 256
MESH = pl.DeviceIdType.MESH
F32 = jnp.float32
BF16 = jnp.bfloat16


def nt(left, right):
    return lax.dot_general(left, right, (((1,), (1,)), ((), ())), preferred_element_type=F32)


def nn(left, right):
    return lax.dot_general(left, right, (((1,), (0,)), ((), ())), preferred_element_type=F32)


def rows_down(values):
    zeros = jnp.zeros((WIDTH, values.shape[1]), values.dtype)
    return jnp.concatenate([zeros, values[: PIXELS - WIDTH]], axis=0)


def rows_up(values):
    zeros = jnp.zeros((WIDTH, values.shape[1]), values.dtype)
    return jnp.concatenate([values[WIDTH:], zeros], axis=0)


def kernel(
    x_ref,
    shard_ref,
    gain_ref,
    shift_ref,
    og_ref,
    mixed_ref,
    ing_ref,
    gt_ref,
    ogr,
    fbuf,
    nbuf,
    wbuf,
    xcol,
    st1,
    st2,
    act_ref,
    actr,
    gsend,
    grecv,
    ysend,
    yrecv,
    n2send,
    n2recv,
    f2send,
    f2recv,
    fin,
    rim_s,
    rim_r,
    far_s,
    far_r,
    near_s,
    near_r,
    p1_s,
    p1_r,
    p2_s,
    p2_r,
    p3_s,
    p3_r,
    st1_s,
    st1_r,
    st2_s,
    st2_r,
    arim_s,
    arim_r,
    ga_s,
    ga_r,
    gy_s,
    gy_r,
    gn_s,
    gn_r,
    gf_s,
    gf_r,
    fin_s,
    fin_r,
):
    f = lax.axis_index("fsdp")
    s = lax.axis_index("seq")
    z = f % NZ
    yh = f // NZ
    c = s % 2
    x = (s // 2) % 4
    yl = s // 8
    y = yh * 2 + yl
    res = z % 8
    oct_ = z // 8

    def copy(src, dst, send, recv, fdev, sdev):
        return pltpu.make_async_remote_copy(
            src_ref=src,
            dst_ref=dst,
            send_sem=send,
            recv_sem=recv,
            device_id=(fdev, sdev),
            device_id_type=MESH,
        )

    def zpeer(d):
        return yh * NZ + (z + d + NZ) % NZ

    barrier = pltpu.get_barrier_semaphore()

    def hello(fdev, sdev):
        pl.semaphore_signal(barrier, inc=1, device_id=(fdev, sdev), device_id_type=MESH)

    for j in range(1, 16):
        hello(f, (s + j) % 16)
    for d in (-4, -3, -2, -1, 1, 2, 3, 4, 8, 16, 24):
        hello(zpeer(d), s)
    other = (f + NZ) % (2 * NZ)
    hello(other, s)
    hello(other, (s + 8) % 16)

    def colblock(xx, yll, cc):
        return (1 - cc) * (4 * yll + xx) + cc * (8 + 2 * xx + yll)

    def wblock(yhh, yll, xx, cc):
        cb = colblock(xx, yll, cc)
        return wbuf.at[
            pl.ds(pl.multiple_of(yhh * 160, 32), 160), pl.ds(pl.multiple_of(cb * BLK, BLK), BLK)
        ]

    mycol = colblock(x, yl, c)
    fbuf[oct_] = shard_ref[:, pl.ds(pl.multiple_of(mycol * BLK, BLK), BLK)]

    pl.semaphore_wait(barrier, 28)

    far = []
    for j in (1, 2, 3):
        cp = copy(fbuf.at[oct_], fbuf.at[oct_], far_s.at[j], far_r.at[j], zpeer(8 * j), s)
        cp.start()
        far.append(cp)
    rim_up = copy(og_ref, ogr.at[0], rim_s.at[0], rim_r.at[0], f, (s + 1) % 16)
    rim_down = copy(og_ref, ogr.at[1], rim_s.at[1], rim_r.at[1], f, (s + 15) % 16)
    rim_up.start()
    rim_down.start()

    def far_in(j):
        src = (oct_ - j + 4) % 4
        return copy(fbuf.at[src], fbuf.at[src], far_s.at[j], far_r.at[j], zpeer(8 * j), s)

    for j in (1, 2, 3):
        far_in(j).wait_recv()
    nbuf[res] = jnp.concatenate([fbuf[m].astype(F32) for m in range(4)], axis=0).astype(BF16)
    near = []
    for n, d in enumerate(NEAR):
        cp = copy(nbuf.at[res], nbuf.at[res], near_s.at[n], near_r.at[n], zpeer(d), s)
        cp.start()
        near.append(cp)

    col = lax.broadcasted_iota(jnp.int32, (HEIGHT, WIDTH, CH), 1).reshape(PIXELS, CH)
    inp = x_ref[...].astype(F32)
    left = jnp.where(col >= 1, pltpu.roll(inp, 1, 0), 0.0)
    right = jnp.where(col <= WIDTH - 2, pltpu.roll(inp, PIXELS - 1, 0), 0.0)
    for b, moved in enumerate((left, inp, right)):
        for a, shifted in enumerate((rows_down(moved), moved, rows_up(moved))):
            at = (3 * a + b) * CH
            xcol[:, at : at + CH] = shifted.astype(BF16)
    xcol[:, 9 * CH :] = jnp.zeros((PIXELS, TIME_AT - 9 * CH), BF16)

    def one_hot(shape, slot_dim):
        slot = lax.broadcasted_iota(jnp.int32, shape, slot_dim)
        row = lax.broadcasted_iota(jnp.int32, shape, 1 - slot_dim)
        within = slot & 7
        target = ((slot >> 5) + (((slot >> 3) & 3) << 3)) * 5 + within
        return jnp.where((target == row) & (within < 5), 1.0, 0.0).astype(BF16)

    for n, d in enumerate(NEAR):
        src = (res - d + 8) % 8
        copy(nbuf.at[src], nbuf.at[src], near_s.at[n], near_r.at[n], zpeer(d), s).wait_recv()
    packed = nn(one_hot((160, 256), 1), nbuf[...].reshape(256, BLK)).astype(BF16)
    wbuf[
        pl.ds(pl.multiple_of(yh * 160, 32), 160), pl.ds(pl.multiple_of(mycol * BLK, BLK), BLK)
    ] = packed

    def dev(yy, xx):
        return (yy // 2) * NZ + z, (yy % 2) * 8 + xx * 2 + c

    def block_of(yy, xx, cc):
        return wblock(yy // 2, yy % 2, xx, cc)

    mine = block_of(y, x, c)
    sib = s + 1 - 2 * c

    def to_sibling(ref, n):
        copy(ref, ref, p3_s.at[n], p3_r.at[n], f, sib).start()

    for j in range(1, 4):
        fd, sd = dev((y + c * j) % 4, (x + (1 - c) * j) % 4)
        copy(mine, mine, p1_s.at[j], p1_r.at[j], fd, sd).start()

    def first_block(i):
        return (y - c * i + 4) % 4, (x - (1 - c) * i + 4) % 4

    for i in range(4):
        by, bx = first_block(i)
        ref = block_of(by, bx, c)
        if i:
            copy(ref, ref, p1_s.at[i], p1_r.at[i], f, sib).wait_recv()
        for j in range(1, 4):
            fd, sd = dev((y + (1 - c) * j) % 4, (x + c * j) % 4)
            copy(ref, ref, p2_s.at[4 * j + i], p2_r.at[4 * j + i], fd, sd).start()
        to_sibling(ref, i)

    def second_block(i, j, cc):
        return (
            (y - (1 - cc) * j - cc * i + 8) % 4,
            (x - cc * j - (1 - cc) * i + 8) % 4,
        )

    for j in range(1, 4):
        for i in range(4):
            by, bx = second_block(i, j, c)
            ref = block_of(by, bx, c)
            copy(ref, ref, p2_s.at[4 * j + i], p2_r.at[4 * j + i], f, sib).wait_recv()
            to_sibling(ref, 4 * j + i)
    for n in range(16):
        by, bx = second_block(n % 4, n // 4, 1 - c)
        ref = block_of(by, bx, 1 - c)
        copy(ref, ref, p3_s.at[n], p3_r.at[n], f, sib).wait_recv()

    hidden = nt(xcol[...], wbuf[:, 0:TIME_AT])
    sums = jnp.concatenate(
        [jnp.sum(hidden, axis=0, keepdims=True), jnp.sum(hidden * hidden, axis=0, keepdims=True)],
        axis=0,
    )

    def exchange(buf, value, send, recv):
        buf[s] = value

        def go(j, carry):
            copy(buf.at[s], buf.at[s], send.at[j], recv.at[j], f, (s + j) % 16).start()
            return carry

        lax.fori_loop(1, 16, go, 0)

    def arrived(buf, send, recv):
        def take(j, carry):
            src = (s - j + 16) % 16
            copy(buf.at[src], buf.at[src], send.at[j], recv.at[j], f, src).wait_recv()
            return carry

        lax.fori_loop(1, 16, take, 0)

    exchange(st1, sums, st1_s, st1_r)

    has_left = jnp.where(s > 0, 1.0, 0.0)
    has_right = jnp.where(s < FRAMES - 1, 1.0, 0.0)
    rim_up.wait_recv()
    rim_down.wait_recv()
    wtime = wbuf[:, TIME_AT:COLS]
    taps = [wtime[:, k * CH : (k + 1) * CH] for k in range(3)]
    act_grad = (
        (nn(ogr[1], taps[0]) * has_right + nn(og_ref[...], taps[1]) + nn(ogr[0], taps[2]) * has_left)
        .astype(BF16)
        .astype(F32)
    )
    og_t = [v.T for v in (ogr[1], og_ref[...], ogr[0])]

    row_i = lax.broadcasted_iota(jnp.int32, (CH, CH), 0)
    col_i = lax.broadcasted_iota(jnp.int32, (CH, CH), 1)
    per = CH // GROUPS
    low = row_i - (row_i % per)
    same = jnp.where((col_i >= low) & (col_i < low + per), 1.0, 0.0)
    counted = float(FRAMES * PIXELS * per)

    def group_means(buf):
        total = jnp.sum(buf[...], axis=0)
        grouped = lax.dot_general(
            total,
            same,
            (((1,), (0,)), ((), ())),
            precision=lax.Precision.HIGHEST,
            preferred_element_type=F32,
        )
        return grouped[0:1] / counted, grouped[1:2] / counted

    arrived(st1, st1_s, st1_r)
    average, squares = group_means(st1)
    inv_std = lax.rsqrt(squares - average * average + EPSILON)
    gain = gain_ref[...]
    normed = (hidden - average) * inv_std
    preact = normed * gain + shift_ref[...]
    sig = 1.0 / (1.0 + jnp.exp(-preact))
    activation = (preact * sig).astype(BF16)
    act_ref[...] = activation

    for k, weight in enumerate((has_right, None, has_left)):
        part = nn(og_t[k], activation)
        if weight is not None:
            part = part * weight
        for b in range(5):
            at = 64 * b
            gsend[5 * k + b] = jnp.concatenate(
                [part[0:160, at : at + 64], part[160:320, at : at + 64]], axis=1
            ).astype(BF16)
    gsend[15] = jnp.zeros((160, 128), BF16)

    def ga_go(j, carry):
        peer = (s + j) % 16
        copy(gsend.at[peer], grecv.at[s], ga_s.at[j], ga_r.at[j], f, peer).start()
        return carry

    lax.fori_loop(1, 16, ga_go, 0)
    grecv[s] = gsend[s]
    arim_up = copy(act_ref, actr.at[0], arim_s.at[0], arim_r.at[0], f, (s + 1) % 16)
    arim_down = copy(act_ref, actr.at[1], arim_s.at[1], arim_r.at[1], f, (s + 15) % 16)
    arim_up.start()
    arim_down.start()

    scaled = act_grad * (sig * (1.0 + preact * (1.0 - sig))) * gain
    back = jnp.concatenate(
        [jnp.sum(scaled, axis=0, keepdims=True), jnp.sum(scaled * normed, axis=0, keepdims=True)],
        axis=0,
    )
    exchange(st2, back, st2_s, st2_r)

    arim_up.wait_recv()
    arim_down.wait_recv()
    mixed_ref[...] = (
        nt(actr[0], taps[0]) * has_left + nt(activation, taps[1]) + nt(actr[1], taps[2]) * has_right
    ).astype(BF16)

    arrived(st2, st2_s, st2_r)
    mean_one, mean_two = group_means(st2)
    hid_grad = (inv_std * (scaled - mean_one - normed * mean_two)).astype(BF16)

    def spread(b):
        parts = [nn(hid_grad, wbuf[:, 0:TIME_AT][:, (3 * a + b) * CH : (3 * a + b + 1) * CH]) for a in range(3)]
        return rows_up(parts[0]) + parts[1] + rows_down(parts[2])

    total = spread(1)
    total = total + jnp.where(col <= WIDTH - 2, pltpu.roll(spread(0), PIXELS - 1, 0), 0.0)
    total = total + jnp.where(col >= 1, pltpu.roll(spread(2), 1, 0), 0.0)
    ing_ref[...] = total.astype(BF16)

    def ga_take(j, carry):
        src = (s - j + 16) % 16
        copy(gsend.at[src], grecv.at[src], ga_s.at[j], ga_r.at[j], f, src).wait_recv()
        return carry

    lax.fori_loop(1, 16, ga_take, 0)
    share = jnp.zeros((160, 128), F32)
    for i in range(16):
        share = share + grecv[i].astype(F32)
    ysend[...] = share.astype(BF16)
    ycopy = copy(ysend, yrecv, gy_s.at[0], gy_r.at[0], other, s)
    ycopy.start()
    ycopy.wait_recv()
    share = share + yrecv[...].astype(F32)
    is_hi = yh.astype(F32)
    share = share * (1.0 - is_hi) + pltpu.roll(share, 64, 1) * is_hi
    n2send[...] = nn(one_hot((256, 160), 0), share.astype(BF16)).astype(BF16).reshape(8, 32, 128)
    for n, d in enumerate(NEAR):
        to = (res + d + 8) % 8
        copy(n2send.at[to], n2recv.at[n], gn_s.at[n], gn_r.at[n], zpeer(d), s).start()
    near_sum = n2send[res].astype(F32)
    for n, d in enumerate(NEAR):
        copy(n2send.at[res], n2recv.at[n], gn_s.at[n], gn_r.at[n], zpeer(d), s).wait_recv()
        near_sum = near_sum + n2recv[n].astype(F32)
    f2send[...] = near_sum.reshape(4, 8, 128)
    for j in (1, 2, 3):
        to = (oct_ + j) % 4
        copy(f2send.at[to], f2recv.at[j], gf_s.at[j], gf_r.at[j], zpeer(8 * j), s).start()
    last = f2send[oct_]
    for j in (1, 2, 3):
        copy(f2send.at[oct_], f2recv.at[j], gf_s.at[j], gf_r.at[j], zpeer(8 * j), s).wait_recv()
        last = last + f2recv[j]
    clips = lax.axis_size("fsdp")
    exchange(fin, last * (1.0 / (clips * FRAMES)), fin_s, fin_r)
    arrived(fin, fin_s, fin_r)
    gt_ref[...] = jnp.concatenate([fin[b][:, 0:64] for b in range(15)], axis=1)[0:5]

    for cp in far + near + [rim_up, rim_down, arim_up, arim_down, ycopy]:
        cp.wait_send()
    for j in range(1, 4):
        copy(mine, mine, p1_s.at[j], p1_r.at[j], f, sib).wait_send()
        for i in range(4):
            by, bx = first_block(i)
            ref = block_of(by, bx, c)
            copy(ref, ref, p2_s.at[4 * j + i], p2_r.at[4 * j + i], f, sib).wait_send()
    for n in range(16):
        by, bx = second_block(n % 4, n // 4, c)
        ref = block_of(by, bx, c)
        copy(ref, ref, p3_s.at[n], p3_r.at[n], f, sib).wait_send()

    def sent(j, carry):
        peer = (s + j) % 16
        copy(st1.at[s], st1.at[s], st1_s.at[j], st1_r.at[j], f, peer).wait_send()
        copy(st2.at[s], st2.at[s], st2_s.at[j], st2_r.at[j], f, peer).wait_send()
        copy(gsend.at[peer], grecv.at[s], ga_s.at[j], ga_r.at[j], f, peer).wait_send()
        copy(fin.at[s], fin.at[s], fin_s.at[j], fin_r.at[j], f, peer).wait_send()
        return carry

    lax.fori_loop(1, 16, sent, 0)
    for n, d in enumerate(NEAR):
        to = (res + d + 8) % 8
        copy(n2send.at[to], n2recv.at[n], gn_s.at[n], gn_r.at[n], zpeer(d), s).wait_send()
    for j in (1, 2, 3):
        to = (oct_ + j) % 4
        copy(f2send.at[to], f2recv.at[j], gf_s.at[j], gf_r.at[j], zpeer(8 * j), s).wait_send()


def local(clips_in, weight_space, weight_time, norm_gain, norm_shift, out_grad):
    shard = jnp.concatenate(
        [
            jnp.pad(weight_space, ((0, 3), (0, TIME_AT - 9 * CH))),
            jnp.pad(weight_time, ((0, 3), (0, COLS - TIME_AT - 3 * CH))),
        ],
        axis=1,
    )
    vmem = pl.BlockSpec(memory_space=pltpu.VMEM)
    dma = pltpu.SemaphoreType.DMA
    mixed, in_grad, grad_time = pl.pallas_call(
        kernel,
        out_shape=(
            jax.ShapeDtypeStruct((PIXELS, CH), BF16),
            jax.ShapeDtypeStruct((PIXELS, CH), BF16),
            jax.ShapeDtypeStruct((5, 3 * CH), F32),
        ),
        in_specs=[vmem] * 5,
        out_specs=(vmem, vmem, vmem),
        scratch_shapes=[
            pltpu.VMEM((2, PIXELS, CH), BF16),
            pltpu.VMEM((4, 8, BLK), BF16),
            pltpu.VMEM((8, 32, BLK), BF16),
            pltpu.VMEM((CH, COLS), BF16),
            pltpu.VMEM((PIXELS, TIME_AT), BF16),
            pltpu.VMEM((16, 2, CH), F32),
            pltpu.VMEM((16, 2, CH), F32),
            pltpu.VMEM((PIXELS, CH), BF16),
            pltpu.VMEM((2, PIXELS, CH), BF16),
            pltpu.VMEM((16, 160, 128), BF16),
            pltpu.VMEM((16, 160, 128), BF16),
            pltpu.VMEM((160, 128), BF16),
            pltpu.VMEM((160, 128), BF16),
            pltpu.VMEM((8, 32, 128), BF16),
            pltpu.VMEM((7, 32, 128), BF16),
            pltpu.VMEM((4, 8, 128), F32),
            pltpu.VMEM((4, 8, 128), F32),
            pltpu.VMEM((16, 8, 128), F32),
        ]
        + [dma((n,)) for n in (2, 2, 4, 4, 7, 7, 4, 4, 16, 16, 16, 16)]
        + [dma((16,))] * 4
        + [dma((2,))] * 2
        + [dma((16,))] * 2
        + [dma((1,))] * 2
        + [dma((7,))] * 2
        + [dma((4,))] * 2
        + [dma((16,))] * 2,
        compiler_params=pltpu.CompilerParams(
            collective_id=0, has_side_effects=True, vmem_limit_bytes=56 * 1024 * 1024
        ),
    )(
        clips_in.reshape(PIXELS, CH),
        shard,
        norm_gain.reshape(1, CH),
        norm_shift.reshape(1, CH),
        out_grad.reshape(PIXELS, CH),
    )
    return mixed.reshape(clips_in.shape), in_grad.reshape(clips_in.shape), grad_time


def solution(mesh):
    in_specs = (
        P("fsdp", "seq", None, None),
        P("fsdp", None),
        P("fsdp", None),
        P(),
        P(),
        P("fsdp", "seq", None, None),
    )
    out_specs = (P("fsdp", "seq", None, None), P("fsdp", "seq", None, None), P("fsdp", None))
    return jax.shard_map(local, mesh=mesh, in_specs=in_specs, out_specs=out_specs, check_vma=False)
```

time: 1040 us -> 125 us (0.12)
  waiting for transfers between devices: 644 us -> 0 us
  blocking collectives: 286 us -> 0 us
  Pallas kernels: 0 us -> 115 us
  local copies, waits for them, and re-layouts: 48 us -> 7.92 us
  starting transfers between devices: 26.6 us -> 0 us
  matrix products: 16 us -> 0 us
  between operations: 15 us -> 0.66 us
    unnamed x3 -> x0, waiting for transfers between devices: 518 us -> none
    psum x2 -> x0, blocking collectives: 159 us -> none  [group_totals(): return lax.psum((first_sums, second_sums), 'seq')]
    all_gather x1 -> x0, blocking collectives: 127 us -> none  [local(): lax.all_gather(weight_time, 'fsdp', axis=0, tiled=True)]
    all_gather x1 -> x0, waiting for transfers between devices: 123 us -> none  [local(): lax.all_gather(weight_space, 'fsdp', axis=0, tiled=True)]
    pallas_call x0 -> x1, Pallas kernels: none -> 115 us  [local(): pl.pallas_call(kernel, out_shape=(jax.ShapeDtypeStruct((PIXELS, CH), BF16...]
    ppermute x4 -> x0, starting transfers between devices: 26.6 us -> none  [the longest x2 20.1 us: extended_2(): after = lax.ppermute(leading, axis, down)]
    dot_general x9 -> x0, matrix products: 16 us -> none  [the longest x3 6.36 us: conv_time_back(): jnp.dot(slab_rows, weight[:, offset * channels:(offset + 1) * channels],...]
    unnamed x45 -> x13, local copies, waits for them, and re-layouts: 19.4 us -> 6.11 us
  transfers between devices with their start and end apart: 6 -> 0, of which waited for: 3 -> 0; matrix products, arithmetic and copies ran while one was open for 3% -> 0% of each run, Pallas kernels for 0% -> 0%
where the time goes in v1:
time: 125 us
  Pallas kernels  115 us (92%)
  local copies, waits for them, and re-layouts  7.92 us (6%)
  other arithmetic  1.46 us (1%)
    pallas_call x1, Pallas kernels, local(): pl.pallas_call(kernel, out_shape=(jax.ShapeDtypeStruct((PIXELS, CH), BF16...  115 us
    unnamed x13, local copies, waits for them, and re-layouts  6.11 us

profile of v1, /device:TPU:1, one launch (start us, length us, event | category | flops | bytes accessed | tf_op | source)
XLA Modules:
  0.0 124.6 jit_solution(8061693234002982603)
XLA Ops:
  0.6 0.0 copy-start.3
  0.6 1.3 %reshape.25.gain_ref = f32[1,320]{1,0:T(1,128)} reshape(f32[320]{0:T(512)} %param.9) | data formatting | bytes 2560 | tf_op jit(solution)/shard_map/reshape | solution.py:479
  1.9 0.0 copy-done.3
  1.9 0.6 reshape.26.shift_ref
  2.5 1.5 %fusion.2.shard_ref = bf16[8,4096]{1,0:T(8,128)(2,1)} fusion(bf16[5,960]{1,0:T(8,128)(2,1)} %param.8, bf16[5,2880]{1,0:T(8,128)(2,1)} %param.7), kind=kLoop, calls=%fused_computation.4 | loop fusion | flops 262144 | bytes 103936 | tf_op jit(solution)/shard_map/concatenate | solution.py:427
  3.9 0.0 copy-start.1
  3.9 1.9 %copy.9 = bf16[1,1,384,320]{3,2,1,0:T(8,128)(2,1)} copy(bf16[1,1,384,320]{2,3,1,0:T(8,128)(2,1)} %param.6) | data formatting | bytes 491520 | tf_op args[0]
  5.8 0.0 copy-done.1
  5.8 0.9 copy.10
  6.7 114.6 %shard_map.85 = (bf16[384,320]{1,0:T(8,128)(2,1)}, bf16[384,320]{1,0:T(8,128)(2,1)}, f32[5,960]{1,0:T(8,128)}) custom-call(bf16[384,320]{1,0:T(8,128)(2,1)} %bitcast.4, bf16[8,4096]{1,0:T(8,128)(2,1)} %fusion.2.shard_ref, f32[1,320]{1,0:T(1,128)} %reshape.25.gain_ref, f32[1,320]{1,0:T(1,128)} %reshape.26.shift_ref, bf16[384,320]{1,0:T(8,128)(2,1)} %bitcast.5), custom_call_target="tpu_custom_call" | custom-call | tf_op jit(solution)/shard_map/pallas_call | solution.py:436
  121.3 0.0 copy-start
  121.3 1.9 %copy.11 = bf16[1,1,384,320]{2,3,1,0:T(8,128)(2,1)} copy(bf16[1,1,384,320]{3,2,1,0:T(8,128)(2,1)} %bitcast.7) | data formatting | bytes 491520
  123.1 0.0 copy-done
  123.1 0.0 copy-start.2
  123.1 0.9 copy.12
  124.0 0.0 copy-done.2
  124.0 0.6 copy.14
Async XLA Ops:
  0.6 1.3 %copy-start.3 = (f32[320]{0:T(512)S(1)}, f32[320]{0:T(512)}, u32[]{:S(2)}) copy-start(f32[320]{0:T(512)} %param.10) | copy-start | bytes 3844
  3.9 1.9 %copy-start.1 = (bf16[1,1,384,320]{2,3,1,0:T(8,128)(2,1)S(1)}, bf16[1,1,384,320]{2,3,1,0:T(8,128)(2,1)}, u32[]{:S(2)}) copy-start(bf16[1,1,384,320]{2,3,1,0:T(8,128)(2,1)} %param.11) | copy-start | bytes 737284
  121.3 1.9 %copy-start = (bf16[384,320]{1,0:T(8,128)(2,1)S(1)}, bf16[384,320]{1,0:T(8,128)(2,1)}, u32[]{:S(2)}) copy-start(bf16[384,320]{1,0:T(8,128)(2,1)} %get-tuple-element.7) | copy-start | bytes 737284
  123.1 0.9 copy-start.2

commit v2 on v1

v2 whole, which is shorter than its diff:
```python
import jax
import jax.numpy as jnp
from jax import lax
from jax.experimental import pallas as pl
from jax.experimental.pallas import tpu as pltpu
from jax.sharding import PartitionSpec as P

GROUPS = 32
FRAMES = 16
HEIGHT = 16
WIDTH = 24
PIXELS = HEIGHT * WIDTH
CH = 320
EPSILON = 1e-05
NZ = 32
TIME_AT = 3072
COLS = 4096
BLK = 256
MESH = pl.DeviceIdType.MESH
F32 = jnp.float32
BF16 = jnp.bfloat16


def nt(left, right):
    return lax.dot_general(left, right, (((1,), (1,)), ((), ())), preferred_element_type=F32)


def nn(left, right):
    return lax.dot_general(left, right, (((1,), (0,)), ((), ())), preferred_element_type=F32)


def flight_order(i):
    half = (i + 1) // 2
    return 16 + half * (1 - 2 * (i % 2))


def kernel(
    x_ref,
    ws_ref,
    wt_ref,
    gain_ref,
    shift_ref,
    og_ref,
    mixed_ref,
    ing_ref,
    gt_ref,
    ogr,
    wpad,
    zbuf,
    wbuf,
    xcol,
    st1,
    st2,
    act_ref,
    actr,
    gall,
    gsib,
    gchip,
    gplane,
    zsend,
    zrecv,
    fval,
    fin,
    wtrans,
    rim_s,
    rim_r,
    zw_s,
    zw_r,
    p1_s,
    p1_r,
    p2_s,
    p2_r,
    p3_s,
    p3_r,
    st1_s,
    st1_r,
    st2_s,
    st2_r,
    arim_s,
    arim_r,
    gc_s,
    gc_r,
    gp_s,
    gp_r,
    gz_s,
    gz_r,
    fin_s,
    fin_r,
):
    f = lax.axis_index("fsdp")
    s = lax.axis_index("seq")
    z = f % NZ
    yh = f // NZ
    c = s % 2
    x = (s // 2) % 4
    yl = s // 8
    y = yh * 2 + yl
    chip = y * 4 + x
    sib = s + 1 - 2 * c
    pending = []

    def copy(src, dst, send, recv, fdev, sdev):
        return pltpu.make_async_remote_copy(
            src_ref=src,
            dst_ref=dst,
            send_sem=send,
            recv_sem=recv,
            device_id=(fdev, sdev),
            device_id_type=MESH,
        )

    def start(cp):
        cp.start()
        pending.append(cp.wait_send)

    def loop(low, high, body):
        def step(i, carry):
            body(i)
            return carry

        lax.fori_loop(low, high, step, 0)

    def zpeer(d):
        return yh * NZ + (z + d) % NZ

    def on_chip(q, cc):
        return (q // 8) * NZ + z, ((q // 4) % 2) * 8 + (q % 4) * 2 + cc

    barrier = pltpu.get_barrier_semaphore()

    def hello(fdev, sdev):
        pl.semaphore_signal(barrier, inc=1, device_id=(fdev, sdev), device_id_type=MESH)

    loop(0, 31, lambda i: hello(zpeer(flight_order(i)), s))

    def hello_plane(j):
        q = (chip + j) % 16
        for cc in (0, 1):
            fd, sd = on_chip(q, cc)
            hello(fd, sd)

    loop(1, 16, hello_plane)
    hello(f, sib)

    def colblock(xx, yll, cc):
        return (1 - cc) * (4 * yll + xx) + cc * (8 + 2 * xx + yll)

    def wblock(yy, xx, cc):
        cb = colblock(xx, yy % 2, cc)
        return wbuf.at[
            pl.ds(pl.multiple_of((yy // 2) * 160, 32), 160),
            pl.ds(pl.multiple_of(cb * BLK, BLK), BLK),
        ]

    mycol = pl.multiple_of(colblock(x, yl, c) * BLK, BLK)
    wpad[...] = jnp.zeros((8, COLS), F32)
    wpad[0:5, 0 : 9 * CH] = ws_ref[...].astype(F32)
    wpad[0:5, TIME_AT : TIME_AT + 3 * CH] = wt_ref[...].astype(F32)
    zbuf[z] = wpad[:, pl.ds(mycol, BLK)].astype(BF16)

    pix = lax.broadcasted_iota(jnp.int32, (1, PIXELS), 1)
    col = pix - WIDTH * ((pix * 2731) >> 16)

    def inside(a, b):
        ok = pix >= 0
        if a == 0:
            ok = ok & (pix >= WIDTH)
        if a == 2:
            ok = ok & (pix < PIXELS - WIDTH)
        if b == 0:
            ok = ok & (col >= 1)
        if b == 2:
            ok = ok & (col <= WIDTH - 2)
        return ok

    def moved(values, a, b):
        step = WIDTH * (a - 1) + b - 1
        if step == 0:
            return values
        return jnp.where(inside(a, b), pltpu.roll(values, (-step) % PIXELS, 1), 0.0)

    inp = x_ref[...].astype(F32)
    for a in range(3):
        for b in range(3):
            at = (3 * a + b) * CH
            xcol[at : at + CH, :] = moved(inp, a, b).astype(BF16)
    xcol[9 * CH :, :] = jnp.zeros((TIME_AT - 9 * CH, PIXELS), BF16)

    pl.semaphore_wait(barrier, 62)

    def zw_copy(d, slot):
        return copy(zbuf.at[slot], zbuf.at[slot], zw_s.at[d], zw_r.at[d], zpeer(d), s)

    loop(0, 31, lambda i: zw_copy(flight_order(i), z).start())
    pending.append(lambda: loop(1, 32, lambda d: zw_copy(d, z).wait_send()))
    rim_up = copy(og_ref, ogr.at[0], rim_s.at[0], rim_r.at[0], f, (s + 1) % 16)
    rim_down = copy(og_ref, ogr.at[1], rim_s.at[1], rim_r.at[1], f, (s + 15) % 16)
    start(rim_up)
    start(rim_down)
    loop(1, 32, lambda d: zw_copy(d, (z - d + NZ) % NZ).wait_recv())

    slot = lax.broadcasted_iota(jnp.int32, (160, 256), 1)
    row = lax.broadcasted_iota(jnp.int32, (160, 256), 0)
    pick = jnp.where(((slot >> 3) * 5 + (slot & 7) == row) & ((slot & 7) < 5), 1.0, 0.0).astype(BF16)
    pieces = zbuf[...].astype(F32).reshape(256, BLK).astype(BF16)
    wbuf[pl.ds(pl.multiple_of(yh * 160, 32), 160), pl.ds(mycol, BLK)] = nn(pick, pieces).astype(BF16)

    def to_sibling(ref, n):
        start(copy(ref, ref, p3_s.at[n], p3_r.at[n], f, sib))

    def first_block(i):
        return (y - c * i + 4) % 4, (x - (1 - c) * i + 4) % 4

    def second_block(i, j, cc):
        return (y - (1 - cc) * j - cc * i + 8) % 4, (x - cc * j - (1 - cc) * i + 8) % 4

    mine = wblock(y, x, c)
    for j in range(1, 4):
        fd, sd = on_chip(((y + c * j) % 4) * 4 + (x + (1 - c) * j) % 4, c)
        start(copy(mine, mine, p1_s.at[j], p1_r.at[j], fd, sd))
    for i in range(4):
        by, bx = first_block(i)
        ref = wblock(by, bx, c)
        if i:
            copy(ref, ref, p1_s.at[i], p1_r.at[i], f, sib).wait_recv()
        for j in range(1, 4):
            fd, sd = on_chip(((y + (1 - c) * j) % 4) * 4 + (x + c * j) % 4, c)
            start(copy(ref, ref, p2_s.at[4 * j + i], p2_r.at[4 * j + i], fd, sd))
        to_sibling(ref, i)
    for i in range(4):
        for j in range(1, 4):
            by, bx = second_block(i, j, c)
            ref = wblock(by, bx, c)
            copy(ref, ref, p2_s.at[4 * j + i], p2_r.at[4 * j + i], f, sib).wait_recv()
            to_sibling(ref, 4 * j + i)
    for n in range(16):
        by, bx = second_block(n % 4, n // 4, 1 - c)
        ref = wblock(by, bx, 1 - c)
        copy(ref, ref, p3_s.at[n], p3_r.at[n], f, sib).wait_recv()

    def lane_sums(values):
        part = values[:, 0:128] + values[:, 128:256] + values[:, 256:384]
        return jnp.sum(part.T, axis=0, keepdims=True)

    def sums_of(first, second):
        return jnp.concatenate([lane_sums(first), lane_sums(second)], axis=0)

    def exchange(buf, value, send, recv):
        buf[s] = value

        def go(j):
            return copy(buf.at[s], buf.at[s], send.at[j], recv.at[j], f, (s + j) % 16)

        loop(1, 16, lambda j: go(j).start())
        pending.append(lambda: loop(1, 16, lambda j: go(j).wait_send()))

    def arrived(buf, send, recv):
        def take(j):
            src = (s - j + 16) % 16
            copy(buf.at[src], buf.at[src], send.at[j], recv.at[j], f, src).wait_recv()

        loop(1, 16, take)

    hidden = nn(wbuf[:, 0:TIME_AT], xcol[...])
    exchange(st1, sums_of(hidden, hidden * hidden), st1_s, st1_r)

    has_left = jnp.where(s > 0, 1.0, 0.0)
    has_right = jnp.where(s < FRAMES - 1, 1.0, 0.0)
    rim_up.wait_recv()
    rim_down.wait_recv()
    wtime = wbuf[:, TIME_AT:COLS]
    taps = [wtime[:, k * CH : (k + 1) * CH] for k in range(3)]
    grads = (ogr[1], og_ref[...], ogr[0])
    act_grad = (
        (
            nn(taps[0].T, grads[0]) * has_right
            + nn(taps[1].T, grads[1])
            + nn(taps[2].T, grads[2]) * has_left
        )
        .astype(BF16)
        .astype(F32)
    )
    per = CH // GROUPS
    row_i = lax.broadcasted_iota(jnp.int32, (CH, CH), 0)
    col_i = lax.broadcasted_iota(jnp.int32, (CH, CH), 1)
    low = row_i - (row_i % per)
    same = jnp.where((col_i >= low) & (col_i < low + per), 1.0, 0.0)
    counted = float(FRAMES * PIXELS * per)

    def group_means(buf):
        grouped = lax.dot_general(
            same,
            jnp.sum(buf[...], axis=0),
            (((1,), (1,)), ((), ())),
            precision=lax.Precision.HIGHEST,
            preferred_element_type=F32,
        )
        return grouped[:, 0:1] / counted, grouped[:, 1:2] / counted

    def column(ref):
        return jnp.broadcast_to(ref[...].reshape(1, CH), (8, CH)).T[:, 0:1]

    gain = column(gain_ref)
    shift = column(shift_ref)

    arrived(st1, st1_s, st1_r)
    average, squares = group_means(st1)
    inv_std = lax.rsqrt(squares - average * average + EPSILON)
    normed = (hidden - average) * inv_std
    preact = normed * gain + shift
    sig = 1.0 / (1.0 + jnp.exp(-preact))
    activation = (preact * sig).astype(BF16)
    act_ref[...] = activation

    for k, weight in enumerate((has_right, None, has_left)):
        part = nt(grads[k], activation)
        if weight is not None:
            part = part * weight
        part = part.astype(BF16)
        for half in range(2):
            for b in range(5):
                at = 64 * b
                gall[half, 5 * k + b] = jnp.concatenate(
                    [
                        part[160 * half : 160 * half + 80, at : at + 64],
                        part[160 * half + 80 : 160 * half + 160, at : at + 64],
                    ],
                    axis=1,
                )
    for half in range(2):
        gall[half, 15] = jnp.zeros((80, 128), BF16)
    core_copy = copy(gall.at[1 - c], gsib, gc_s.at[0], gc_r.at[0], f, sib)
    start(core_copy)

    scaled = act_grad * (sig * (1.0 + preact * (1.0 - sig))) * gain
    exchange(st2, sums_of(scaled, scaled * normed), st2_s, st2_r)

    core_copy.wait_recv()
    gchip[...] = (gall[c].astype(F32) + gsib[...].astype(F32)).astype(BF16)

    def gp_copy(j, to, src):
        fd, sd = on_chip(to, c)
        return copy(gchip.at[to], gplane.at[src], gp_s.at[j], gp_r.at[j], fd, sd)

    loop(1, 16, lambda j: gp_copy(j, (chip + j) % 16, chip).start())
    pending.append(lambda: loop(1, 16, lambda j: gp_copy(j, (chip + j) % 16, chip).wait_send()))
    gplane[chip] = gchip[chip]
    arim_up = copy(act_ref, actr.at[0], arim_s.at[0], arim_r.at[0], f, (s + 1) % 16)
    arim_down = copy(act_ref, actr.at[1], arim_s.at[1], arim_r.at[1], f, (s + 15) % 16)
    start(arim_up)
    start(arim_down)

    arrived(st2, st2_s, st2_r)
    mean_one, mean_two = group_means(st2)
    hid_grad = (inv_std * (scaled - mean_one - normed * mean_two)).astype(BF16)

    def gp_take(j):
        src = (chip - j + 16) % 16
        gp_copy(j, src, src).wait_recv()

    loop(1, 16, gp_take)
    share = jnp.zeros((80, 128), F32)
    for i in range(16):
        share = share + gplane[i].astype(F32)

    slot = lax.broadcasted_iota(jnp.int32, (128, 80), 0)
    row = lax.broadcasted_iota(jnp.int32, (128, 80), 1)
    put = jnp.where(((slot >> 3) * 5 + (slot & 7) == row) & ((slot & 7) < 5), 1.0, 0.0).astype(BF16)
    zsend[...] = nn(put, share.astype(BF16)).reshape(16, 8, 128).astype(BF16)

    def gz_copy(d):
        return copy(zsend.at[(z + d) % 16], zrecv.at[d], gz_s.at[d], gz_r.at[d], zpeer(d), s)

    loop(0, 31, lambda i: gz_copy(flight_order(i)).start())
    pending.append(lambda: loop(1, 32, lambda d: gz_copy(d).wait_send()))
    zrecv[0] = zsend[z % 16]

    wtrans[...] = wbuf[:, 0:TIME_AT].T
    total = nn(wtrans[4 * CH : 5 * CH, :], hid_grad)
    for a in range(3):
        for b in range(3):
            if a != 1 or b != 1:
                at = (3 * a + b) * CH
                total = total + moved(nn(wtrans[at : at + CH, :], hid_grad), 2 - a, 2 - b)
    ing_ref[...] = total.astype(BF16)
    arim_up.wait_recv()
    arim_down.wait_recv()
    mixed_ref[...] = (
        nn(taps[0], actr[0]) * has_left + nn(taps[1], act_ref[...]) + nn(taps[2], actr[1]) * has_right
    ).astype(BF16)

    loop(1, 32, lambda d: gz_copy(d).wait_recv())
    last = jnp.sum(zrecv[...].astype(F32), axis=0)
    right = jnp.where(z >= 16, 1.0, 0.0)
    last = last * (1.0 - right) + pltpu.roll(last, 64, 1) * right
    fval[...] = last * (1.0 / (lax.axis_size("fsdp") * FRAMES))

    def fin_copy(j, src):
        return copy(fval, fin.at[src], fin_s.at[j], fin_r.at[src], c * NZ + z, (s + j) % 16)

    @pl.when(yh == c)
    def _():
        fin[chip] = fval[...]

    @pl.when(yh != c)
    def _():
        fin_copy(0, chip).start()

    loop(1, 16, lambda j: fin_copy(j, chip).start())

    def fin_take(src):
        @pl.when((yh != c) | (src != chip))
        def _():
            fin_copy(0, src).wait_recv()

    loop(0, 16, fin_take)
    gt_ref[...] = jnp.concatenate([fin[b][:, 0:64] for b in range(15)], axis=1)[0:5]

    @pl.when(yh != c)
    def _():
        fin_copy(0, chip).wait_send()

    loop(1, 16, lambda j: fin_copy(j, chip).wait_send())
    for left_over in pending:
        left_over()


def local(clips_in, weight_space, weight_time, norm_gain, norm_shift, out_grad):
    vmem = pl.BlockSpec(memory_space=pltpu.VMEM)
    dma = pltpu.SemaphoreType.DMA
    mixed, in_grad, grad_time = pl.pallas_call(
        kernel,
        out_shape=(
            jax.ShapeDtypeStruct((CH, PIXELS), BF16),
            jax.ShapeDtypeStruct((CH, PIXELS), BF16),
            jax.ShapeDtypeStruct((5, 3 * CH), F32),
        ),
        in_specs=[vmem] * 6,
        out_specs=(vmem, vmem, vmem),
        scratch_shapes=[
            pltpu.VMEM((2, CH, PIXELS), BF16),
            pltpu.VMEM((8, COLS), F32),
            pltpu.VMEM((NZ, 8, BLK), BF16),
            pltpu.VMEM((CH, COLS), BF16),
            pltpu.VMEM((TIME_AT, PIXELS), BF16),
            pltpu.VMEM((16, 2, CH), F32),
            pltpu.VMEM((16, 2, CH), F32),
            pltpu.VMEM((CH, PIXELS), BF16),
            pltpu.VMEM((2, CH, PIXELS), BF16),
            pltpu.VMEM((2, 16, 80, 128), BF16),
            pltpu.VMEM((16, 80, 128), BF16),
            pltpu.VMEM((16, 80, 128), BF16),
            pltpu.VMEM((16, 80, 128), BF16),
            pltpu.VMEM((16, 8, 128), BF16),
            pltpu.VMEM((NZ, 8, 128), BF16),
            pltpu.VMEM((8, 128), F32),
            pltpu.VMEM((16, 8, 128), F32),
            pltpu.VMEM((TIME_AT, CH), BF16),
        ]
        + [dma((n,)) for n in (2, 2, NZ, NZ, 4, 4)]
        + [dma((16,))] * 8
        + [dma((2,))] * 2
        + [dma((1,))] * 2
        + [dma((16,))] * 2
        + [dma((NZ,))] * 2
        + [dma((16,))] * 2,
        compiler_params=pltpu.CompilerParams(
            collective_id=0, has_side_effects=True, vmem_limit_bytes=56 * 1024 * 1024
        ),
    )(
        clips_in.reshape(PIXELS, CH).T,
        weight_space,
        weight_time,
        norm_gain,
        norm_shift,
        out_grad.reshape(PIXELS, CH).T,
    )
    return mixed.T.reshape(clips_in.shape), in_grad.T.reshape(clips_in.shape), grad_time


def solution(mesh):
    in_specs = (
        P("fsdp", "seq", None, None),
        P("fsdp", None),
        P("fsdp", None),
        P(),
        P(),
        P("fsdp", "seq", None, None),
    )
    out_specs = (P("fsdp", "seq", None, None), P("fsdp", "seq", None, None), P("fsdp", None))
    return jax.shard_map(local, mesh=mesh, in_specs=in_specs, out_specs=out_specs, check_vma=False)
```

time: 125 us -> 105 us (0.84)
  Pallas kernels: 115 us -> 101 us
  local copies, waits for them, and re-layouts: 7.92 us -> 3.08 us
  other arithmetic: 1.46 us -> 0 us
    pallas_call x1, Pallas kernels: 115 us -> 101 us  [local(): pl.pallas_call(kernel, out_shape=(jax.ShapeDtypeStruct((CH, PIXELS), BF16...]
    unnamed x13 -> x7, local copies, waits for them, and re-layouts: 6.11 us -> 3.08 us
    reshape x2 -> x0, local copies, waits for them, and re-layouts: 1.81 us -> none  [the longest x1 1.25 us: local(): norm_gain.reshape(1, CH)]
    concatenate x1 -> x0, other arithmetic: 1.46 us -> none  [local(): jnp.concatenate([jnp.pad(weight_space, ((0, 3), (0, TIME_AT - 9 * CH))),...]
where the time goes in v2:
time: 105 us
  Pallas kernels  101 us (96%)
  local copies, waits for them, and re-layouts  3.08 us (3%)
    pallas_call x1, Pallas kernels, local(): pl.pallas_call(kernel, out_shape=(jax.ShapeDtypeStruct((CH, PIXELS), BF16...  101 us
    unnamed x7, local copies, waits for them, and re-layouts  3.08 us

profile of v2, /device:TPU:1, one launch (start us, length us, event | category | flops | bytes accessed | tf_op | source)
XLA Modules:
  0.0 105.0 jit_solution(13495237762508479828)
XLA Ops:
  0.6 101.2 %shard_map.85 = (bf16[320,384]{1,0:T(8,128)(2,1)}, bf16[320,384]{1,0:T(8,128)(2,1)}, f32[5,960]{1,0:T(8,128)}) custom-call(bf16[320,384]{1,0:T(8,128)(2,1)} %bitcast.12, bf16[5,2880]{1,0:T(8,128)(2,1)} %ws_ref.1, bf16[5,960]{1,0:T(8,128)(2,1)} %wt_ref.1, f32[320]{0:T(512)} %gain_ref.1, f32[320]{0:T(512)} %shift_ref.1, bf16[320,384]{1,0:T(8,128)(2,1)} %bitcast.13), custom_call_target="tpu_custom_call" | custom-call | tf_op jit(solution)/shard_map/pallas_call | solution.py:431
  101.9 0.0 copy-start
  101.9 1.7 %copy.12 = bf16[1,1,384,320]{2,3,1,0:T(8,128)(2,1)} copy(bf16[1,1,384,320]{2,3,1,0:T(8,128)(2,1)} %bitcast.15) | data formatting | bytes 491520
  103.6 0.0 copy-done
  103.6 0.0 copy-start.1
  103.6 0.7 copy.13
  104.3 0.1 copy-done.1
  104.3 0.6 copy.14
Async XLA Ops:
  101.9 1.7 %copy-start = (bf16[320,384]{1,0:T(8,128)(2,1)S(1)}, bf16[320,384]{1,0:T(8,128)(2,1)}, u32[]{:S(2)}) copy-start(bf16[320,384]{1,0:T(8,128)(2,1)} %get-tuple-element.7) | copy-start | bytes 737284
  103.6 0.8 copy-start.1

commit v3 on v2

--- a/solution.py
+++ b/solution.py
@@ -35,11 +35,18 @@
 
 
 def kernel(
+    x_hbm,
+    ws_hbm,
+    wt_hbm,
+    gain_ref,
+    shift_ref,
+    og_hbm,
+    mixed_hbm,
+    ing_hbm,
+    gt_hbm,
     x_ref,
     ws_ref,
     wt_ref,
-    gain_ref,
-    shift_ref,
     og_ref,
     mixed_ref,
     ing_ref,
@@ -53,7 +60,7 @@
     st2,
     act_ref,
     actr,
-    gall,
+    gout,
     gsib,
     gchip,
     gplane,
@@ -86,6 +93,8 @@
     gz_r,
     fin_s,
     fin_r,
+    in_sem,
+    out_sem,
 ):
     f = lax.axis_index("fsdp")
     s = lax.axis_index("seq")
@@ -99,6 +108,15 @@
     sib = s + 1 - 2 * c
     pending = []
 
+    loads = [
+        pltpu.make_async_copy(src, dst, in_sem.at[n])
+        for n, (src, dst) in enumerate(
+            ((ws_hbm, ws_ref), (wt_hbm, wt_ref), (x_hbm, x_ref), (og_hbm, og_ref))
+        )
+    ]
+    for load in loads:
+        load.start()
+
     def copy(src, dst, send, recv, fdev, sdev):
         return pltpu.make_async_remote_copy(
             src_ref=src,
@@ -154,6 +172,8 @@
 
     mycol = pl.multiple_of(colblock(x, yl, c) * BLK, BLK)
     wpad[...] = jnp.zeros((8, COLS), F32)
+    loads[0].wait()
+    loads[1].wait()
     wpad[0:5, 0 : 9 * CH] = ws_ref[...].astype(F32)
     wpad[0:5, TIME_AT : TIME_AT + 3 * CH] = wt_ref[...].astype(F32)
     zbuf[z] = wpad[:, pl.ds(mycol, BLK)].astype(BF16)
@@ -179,6 +199,7 @@
             return values
         return jnp.where(inside(a, b), pltpu.roll(values, (-step) % PIXELS, 1), 0.0)
 
+    loads[2].wait()
     inp = x_ref[...].astype(F32)
     for a in range(3):
         for b in range(3):
@@ -186,6 +207,7 @@
             xcol[at : at + CH, :] = moved(inp, a, b).astype(BF16)
     xcol[9 * CH :, :] = jnp.zeros((TIME_AT - 9 * CH, PIXELS), BF16)
 
+    loads[3].wait()
     pl.semaphore_wait(barrier, 62)
 
     def zw_copy(d, slot):
@@ -312,39 +334,39 @@
     activation = (preact * sig).astype(BF16)
     act_ref[...] = activation
 
-    for k, weight in enumerate((has_right, None, has_left)):
-        part = nt(grads[k], activation)
-        if weight is not None:
-            part = part * weight
-        part = part.astype(BF16)
-        for half in range(2):
-            for b in range(5):
-                at = 64 * b
-                gall[half, 5 * k + b] = jnp.concatenate(
-                    [
-                        part[160 * half : 160 * half + 80, at : at + 64],
-                        part[160 * half + 80 : 160 * half + 160, at : at + 64],
-                    ],
-                    axis=1,
-                )
-    for half in range(2):
-        gall[half, 15] = jnp.zeros((80, 128), BF16)
-    core_copy = copy(gall.at[1 - c], gsib, gc_s.at[0], gc_r.at[0], f, sib)
+    def share_of(part):
+        pieces = []
+        for k, weight in enumerate((has_right, None, has_left)):
+            ref = (ogr.at[1], og_ref, ogr.at[0])[k]
+            rows = jnp.concatenate(
+                [ref[pl.ds(pl.multiple_of(160 * h + 80 * part, 16), 80), :] for h in range(2)], axis=0
+            )
+            piece = nt(rows, activation)
+            pieces.append(piece if weight is None else piece * weight)
+        pieces.append(jnp.zeros((160, 64), F32))
+        return jnp.concatenate(pieces, axis=1).reshape(2, 80, 1024)
+
+    gout[...] = share_of(1 - c).astype(BF16)
+    core_copy = copy(gout, gsib, gc_s.at[0], gc_r.at[0], f, sib)
     start(core_copy)
+    own_share = share_of(c)
+
+    core_copy.wait_recv()
+    gchip[...] = (own_share + gsib[...].astype(F32)).astype(BF16)
+
+    def tile_of(q):
+        return gchip.at[q // 8, :, pl.ds(pl.multiple_of((q % 8) * 128, 128), 128)]
+
+    def gp_copy(j, to, src):
+        fd, sd = on_chip(to, c)
+        return copy(tile_of(to), gplane.at[src], gp_s.at[j], gp_r.at[j], fd, sd)
+
+    loop(1, 16, lambda j: gp_copy(j, (chip + j) % 16, chip).start())
+    pending.append(lambda: loop(1, 16, lambda j: gp_copy(j, (chip + j) % 16, chip).wait_send()))
+    gplane[chip] = gchip[chip // 8, :, pl.ds(pl.multiple_of((chip % 8) * 128, 128), 128)]
 
     scaled = act_grad * (sig * (1.0 + preact * (1.0 - sig))) * gain
     exchange(st2, sums_of(scaled, scaled * normed), st2_s, st2_r)
-
-    core_copy.wait_recv()
-    gchip[...] = (gall[c].astype(F32) + gsib[...].astype(F32)).astype(BF16)
-
-    def gp_copy(j, to, src):
-        fd, sd = on_chip(to, c)
-        return copy(gchip.at[to], gplane.at[src], gp_s.at[j], gp_r.at[j], fd, sd)
-
-    loop(1, 16, lambda j: gp_copy(j, (chip + j) % 16, chip).start())
-    pending.append(lambda: loop(1, 16, lambda j: gp_copy(j, (chip + j) % 16, chip).wait_send()))
-    gplane[chip] = gchip[chip]
     arim_up = copy(act_ref, actr.at[0], arim_s.at[0], arim_r.at[0], f, (s + 1) % 16)
     arim_down = copy(act_ref, actr.at[1], arim_s.at[1], arim_r.at[1], f, (s + 15) % 16)
     start(arim_up)
@@ -367,13 +389,18 @@
     row = lax.broadcasted_iota(jnp.int32, (128, 80), 1)
     put = jnp.where(((slot >> 3) * 5 + (slot & 7) == row) & ((slot & 7) < 5), 1.0, 0.0).astype(BF16)
     zsend[...] = nn(put, share.astype(BF16)).reshape(16, 8, 128).astype(BF16)
+    owner = z // 16 == c
 
     def gz_copy(d):
         return copy(zsend.at[(z + d) % 16], zrecv.at[d], gz_s.at[d], gz_r.at[d], zpeer(d), s)
 
-    loop(0, 31, lambda i: gz_copy(flight_order(i)).start())
-    pending.append(lambda: loop(1, 32, lambda d: gz_copy(d).wait_send()))
-    zrecv[0] = zsend[z % 16]
+    def to_owner(d, act):
+        @pl.when(((z + d) % NZ) // 16 == c)
+        def _():
+            act(gz_copy(d))
+
+    loop(0, 31, lambda i: to_owner(flight_order(i), lambda cp: cp.start()))
+    pending.append(lambda: loop(1, 32, lambda d: to_owner(d, lambda cp: cp.wait_send())))
 
     wtrans[...] = wbuf[:, 0:TIME_AT].T
     total = nn(wtrans[4 * CH : 5 * CH, :], hid_grad)
@@ -383,61 +410,82 @@
                 at = (3 * a + b) * CH
                 total = total + moved(nn(wtrans[at : at + CH, :], hid_grad), 2 - a, 2 - b)
     ing_ref[...] = total.astype(BF16)
+    ing_out = pltpu.make_async_copy(ing_ref, ing_hbm, out_sem.at[0])
+    ing_out.start()
     arim_up.wait_recv()
     arim_down.wait_recv()
     mixed_ref[...] = (
         nn(taps[0], actr[0]) * has_left + nn(taps[1], act_ref[...]) + nn(taps[2], actr[1]) * has_right
     ).astype(BF16)
 
-    loop(1, 32, lambda d: gz_copy(d).wait_recv())
-    last = jnp.sum(zrecv[...].astype(F32), axis=0)
-    right = jnp.where(z >= 16, 1.0, 0.0)
-    last = last * (1.0 - right) + pltpu.roll(last, 64, 1) * right
-    fval[...] = last * (1.0 / (lax.axis_size("fsdp") * FRAMES))
+    mixed_out = pltpu.make_async_copy(mixed_ref, mixed_hbm, out_sem.at[1])
+    mixed_out.start()
 
     def fin_copy(j, src):
-        return copy(fval, fin.at[src], fin_s.at[j], fin_r.at[src], c * NZ + z, (s + j) % 16)
-
-    @pl.when(yh == c)
+        return copy(fval, fin.at[src], fin_s.at[j], fin_r.at[src], f, (s + j) % 16)
+
+    @pl.when(owner)
     def _():
-        fin[chip] = fval[...]
-
-    @pl.when(yh != c)
+        zrecv[0] = zsend[z % 16]
+        loop(1, 32, lambda d: gz_copy(d).wait_recv())
+        last = jnp.sum(zrecv[...].astype(F32), axis=0) * (1.0 / (lax.axis_size("fsdp") * FRAMES))
+        fval[...] = last
+        loop(1, 16, lambda j: fin_copy(j, chip % 8).start())
+        fin[chip % 8] = last
+
+    def fin_take(src):
+        @pl.when(jnp.logical_not(owner) | (src != chip % 8))
+        def _():
+            fin_copy(1, src).wait_recv()
+
+    loop(0, 8, fin_take)
+    gt_ref[...] = jnp.concatenate([fin[t] for t in range(8)], axis=1)[0:5, 0 : 3 * CH]
+    gt_out = pltpu.make_async_copy(gt_ref, gt_hbm, out_sem.at[2])
+    gt_out.start()
+
+    @pl.when(owner)
     def _():
-        fin_copy(0, chip).start()
-
-    loop(1, 16, lambda j: fin_copy(j, chip).start())
-
-    def fin_take(src):
-        @pl.when((yh != c) | (src != chip))
-        def _():
-            fin_copy(0, src).wait_recv()
-
-    loop(0, 16, fin_take)
-    gt_ref[...] = jnp.concatenate([fin[b][:, 0:64] for b in range(15)], axis=1)[0:5]
-
-    @pl.when(yh != c)
-    def _():
-        fin_copy(0, chip).wait_send()
-
-    loop(1, 16, lambda j: fin_copy(j, chip).wait_send())
+        loop(1, 16, lambda j: fin_copy(j, chip % 8).wait_send())
+
     for left_over in pending:
         left_over()
+    ing_out.wait()
+    mixed_out.wait()
+    gt_out.wait()
+
+
+def hand_over(mixed_in, ing_in, gt_in, mixed_out, ing_out, gt_out, sems):
+    copies = [
+        pltpu.make_async_copy(src, dst, sems.at[n])
+        for n, (src, dst) in enumerate(((mixed_in, mixed_out), (ing_in, ing_out), (gt_in, gt_out)))
+    ]
+    for cp in copies:
+        cp.start()
+    for cp in copies:
+        cp.wait()
 
 
 def local(clips_in, weight_space, weight_time, norm_gain, norm_shift, out_grad):
     vmem = pl.BlockSpec(memory_space=pltpu.VMEM)
     dma = pltpu.SemaphoreType.DMA
-    mixed, in_grad, grad_time = pl.pallas_call(
+    hbm = pl.BlockSpec(memory_space=pl.ANY)
+    results = pl.pallas_call(
         kernel,
         out_shape=(
             jax.ShapeDtypeStruct((CH, PIXELS), BF16),
             jax.ShapeDtypeStruct((CH, PIXELS), BF16),
             jax.ShapeDtypeStruct((5, 3 * CH), F32),
         ),
-        in_specs=[vmem] * 6,
-        out_specs=(vmem, vmem, vmem),
+        in_specs=[hbm, hbm, hbm, vmem, vmem, hbm],
+        out_specs=(hbm, hbm, hbm),
         scratch_shapes=[
+            pltpu.VMEM((CH, PIXELS), BF16),
+            pltpu.VMEM((5, 9 * CH), BF16),
+            pltpu.VMEM((5, 3 * CH), BF16),
+            pltpu.VMEM((CH, PIXELS), BF16),
+            pltpu.VMEM((CH, PIXELS), BF16),
+            pltpu.VMEM((CH, PIXELS), BF16),
+            pltpu.VMEM((5, 3 * CH), F32),
             pltpu.VMEM((2, CH, PIXELS), BF16),
             pltpu.VMEM((8, COLS), F32),
             pltpu.VMEM((NZ, 8, BLK), BF16),
@@ -447,14 +495,14 @@
             pltpu.VMEM((16, 2, CH), F32),
             pltpu.VMEM((CH, PIXELS), BF16),
             pltpu.VMEM((2, CH, PIXELS), BF16),
-            pltpu.VMEM((2, 16, 80, 128), BF16),
-            pltpu.VMEM((16, 80, 128), BF16),
-            pltpu.VMEM((16, 80, 128), BF16),
+            pltpu.VMEM((2, 80, 1024), BF16),
+            pltpu.VMEM((2, 80, 1024), BF16),
+            pltpu.VMEM((2, 80, 1024), BF16),
             pltpu.VMEM((16, 80, 128), BF16),
             pltpu.VMEM((16, 8, 128), BF16),
             pltpu.VMEM((NZ, 8, 128), BF16),
             pltpu.VMEM((8, 128), F32),
-            pltpu.VMEM((16, 8, 128), F32),
+            pltpu.VMEM((8, 8, 128), F32),
             pltpu.VMEM((TIME_AT, CH), BF16),
         ]
         + [dma((n,)) for n in (2, 2, NZ, NZ, 4, 4)]
@@ -463,7 +511,7 @@
         + [dma((1,))] * 2
         + [dma((16,))] * 2
         + [dma((NZ,))] * 2
-        + [dma((16,))] * 2,
+        + [dma((16,)), dma((8,)), dma((4,)), dma((3,))],
         compiler_params=pltpu.CompilerParams(
             collective_id=0, has_side_effects=True, vmem_limit_bytes=56 * 1024 * 1024
         ),
@@ -475,6 +523,13 @@
         norm_shift,
         out_grad.reshape(PIXELS, CH).T,
     )
+    mixed, in_grad, grad_time = pl.pallas_call(
+        hand_over,
+        out_shape=tuple(jax.ShapeDtypeStruct(v.shape, v.dtype) for v in results),
+        in_specs=[hbm] * 3,
+        out_specs=(hbm,) * 3,
+        scratch_shapes=[dma((3,))],
+    )(*results)
     return mixed.T.reshape(clips_in.shape), in_grad.T.reshape(clips_in.shape), grad_time
 
 

time: 105 us -> 118 us (1.12)
  Pallas kernels: 101 us -> 117 us
  local copies, waits for them, and re-layouts: 3.08 us -> 0 us
    pallas_call x0 -> x1, Pallas kernels: none -> 17 us  [local(): pl.pallas_call(hand_over, out_shape=tuple((jax.ShapeDtypeStruct(v.shape,...]
    unnamed x7 -> x0, local copies, waits for them, and re-layouts: 3.08 us -> none
    pallas_call x1, Pallas kernels: 101 us -> 100 us  [local(): pl.pallas_call(kernel, out_shape=(jax.ShapeDtypeStruct((CH, PIXELS), BF16...]
where the time goes in v3:
time: 118 us
  Pallas kernels  117 us (99%)
    pallas_call x1, Pallas kernels, local(): pl.pallas_call(kernel, out_shape=(jax.ShapeDtypeStruct((CH, PIXELS), BF16...  100 us
    pallas_call x1, Pallas kernels, local(): pl.pallas_call(hand_over, out_shape=tuple((jax.ShapeDtypeStruct(v.shape,...  17 us

profile of v3, /device:TPU:1, one launch (start us, length us, event | category | flops | bytes accessed | tf_op | source)
XLA Modules:
  0.0 117.7 jit_solution(16555725368877413001)
XLA Ops:
  0.6 100.0 %shard_map.85 = (bf16[320,384]{1,0:T(8,128)(2,1)}, bf16[320,384]{1,0:T(8,128)(2,1)}, f32[5,960]{1,0:T(8,128)}) custom-call(bf16[320,384]{1,0:T(8,128)(2,1)} %bitcast.12, bf16[5,2880]{1,0:T(8,128)(2,1)} %ws_hbm.1, bf16[5,960]{1,0:T(8,128)(2,1)} %wt_hbm.1, f32[320]{0:T(512)} %gain_ref.1, f32[320]{0:T(512)} %shift_ref.1, bf16[320,384]{1,0:T(8,128)(2,1)} %bitcast.13), custom_call_target="tpu_custom_call" | custom-call | tf_op jit(solution)/shard_map/pallas_call | solution.py:472
  100.7 17.0 %shard_map.86 = (bf16[320,384]{1,0:T(8,128)(2,1)}, bf16[320,384]{1,0:T(8,128)(2,1)}, f32[5,960]{1,0:T(8,128)}) custom-call(bf16[320,384]{1,0:T(8,128)(2,1)} %get-tuple-element.9.mixed_in, bf16[320,384]{1,0:T(8,128)(2,1)} %get-tuple-element.10.ing_in, f32[5,960]{1,0:T(8,128)} %get-tuple-element.11.gt_in), custom_call_target="tpu_custom_call" | custom-call | tf_op jit(solution)/shard_map/pallas_call | solution.py:526

commit v4 on v3

--- a/solution.py
+++ b/solution.py
@@ -38,8 +38,8 @@
     x_hbm,
     ws_hbm,
     wt_hbm,
-    gain_ref,
-    shift_ref,
+    gain_hbm,
+    shift_hbm,
     og_hbm,
     mixed_hbm,
     ing_hbm,
@@ -47,6 +47,8 @@
     x_ref,
     ws_ref,
     wt_ref,
+    gain_ref,
+    shift_ref,
     og_ref,
     mixed_ref,
     ing_ref,
@@ -111,7 +113,14 @@
     loads = [
         pltpu.make_async_copy(src, dst, in_sem.at[n])
         for n, (src, dst) in enumerate(
-            ((ws_hbm, ws_ref), (wt_hbm, wt_ref), (x_hbm, x_ref), (og_hbm, og_ref))
+            (
+                (ws_hbm, ws_ref),
+                (wt_hbm, wt_ref),
+                (x_hbm, x_ref),
+                (og_hbm, og_ref),
+                (gain_hbm, gain_ref),
+                (shift_hbm, shift_ref),
+            )
         )
     ]
     for load in loads:
@@ -161,7 +170,8 @@
     hello(f, sib)
 
     def colblock(xx, yll, cc):
-        return (1 - cc) * (4 * yll + xx) + cc * (8 + 2 * xx + yll)
+        last = xx // 3
+        return (1 - last) * (6 * cc + 3 * yll + xx) + last * (12 + 2 * cc + yll)
 
     def wblock(yy, xx, cc):
         cb = colblock(xx, yy % 2, cc)
@@ -207,7 +217,8 @@
             xcol[at : at + CH, :] = moved(inp, a, b).astype(BF16)
     xcol[9 * CH :, :] = jnp.zeros((TIME_AT - 9 * CH, PIXELS), BF16)
 
-    loads[3].wait()
+    for load in loads[3:]:
+        load.wait()
     pl.semaphore_wait(barrier, 62)
 
     def zw_copy(d, slot):
@@ -227,8 +238,16 @@
     pieces = zbuf[...].astype(F32).reshape(256, BLK).astype(BF16)
     wbuf[pl.ds(pl.multiple_of(yh * 160, 32), 160), pl.ds(mycol, BLK)] = nn(pick, pieces).astype(BF16)
 
-    def to_sibling(ref, n):
-        start(copy(ref, ref, p3_s.at[n], p3_r.at[n], f, sib))
+    def to_sibling(i, j):
+        ref = wblock(*second_block(i, j, c), c)
+        n = 4 * j + i
+        return copy(ref, ref, p3_s.at[n], p3_r.at[n], f, sib)
+
+    def onward(i, j):
+        ref = wblock(*first_block(i), c)
+        n = 4 * j + i
+        fd, sd = on_chip(((y + (1 - c) * j) % 4) * 4 + (x + c * j) % 4, c)
+        return copy(ref, ref, p2_s.at[n], p2_r.at[n], fd, sd)
 
     def first_block(i):
         return (y - c * i + 4) % 4, (x - (1 - c) * i + 4) % 4
@@ -240,25 +259,50 @@
     for j in range(1, 4):
         fd, sd = on_chip(((y + c * j) % 4) * 4 + (x + (1 - c) * j) % 4, c)
         start(copy(mine, mine, p1_s.at[j], p1_r.at[j], fd, sd))
+    def forward(i):
+        for j in range(1, 4):
+            onward(i, j).start()
+        to_sibling(i, 0).start()
+
     for i in range(4):
-        by, bx = first_block(i)
-        ref = wblock(by, bx, c)
         if i:
+            ref = wblock(*first_block(i), c)
             copy(ref, ref, p1_s.at[i], p1_r.at[i], f, sib).wait_recv()
-        for j in range(1, 4):
-            fd, sd = on_chip(((y + (1 - c) * j) % 4) * 4 + (x + c * j) % 4, c)
-            start(copy(ref, ref, p2_s.at[4 * j + i], p2_r.at[4 * j + i], fd, sd))
-        to_sibling(ref, i)
+        pl.when(first_block(i)[1] < 3)(lambda i=i: forward(i))
     for i in range(4):
-        for j in range(1, 4):
-            by, bx = second_block(i, j, c)
-            ref = wblock(by, bx, c)
-            copy(ref, ref, p2_s.at[4 * j + i], p2_r.at[4 * j + i], f, sib).wait_recv()
-            to_sibling(ref, 4 * j + i)
-    for n in range(16):
-        by, bx = second_block(n % 4, n // 4, 1 - c)
-        ref = wblock(by, bx, 1 - c)
+        pl.when(first_block(i)[1] == 3)(lambda i=i: forward(i))
+
+    def second(i, j):
+        ref = wblock(*second_block(i, j, c), c)
+        n = 4 * j + i
+        copy(ref, ref, p2_s.at[n], p2_r.at[n], f, sib).wait_recv()
+        to_sibling(i, j).start()
+
+    def from_sibling(i, j):
+        ref = wblock(*second_block(i, j, 1 - c), 1 - c)
+        n = 4 * j + i
         copy(ref, ref, p3_s.at[n], p3_r.at[n], f, sib).wait_recv()
+
+    def take_blocks(temporal):
+        def wanted(bx):
+            return bx == 3 if temporal else bx < 3
+
+        for i in range(4):
+            for j in range(1, 4):
+                pl.when(wanted(second_block(i, j, c)[1]))(lambda i=i, j=j: second(i, j))
+        for i in range(4):
+            for j in range(4):
+                pl.when(wanted(second_block(i, j, 1 - c)[1]))(lambda i=i, j=j: from_sibling(i, j))
+
+    def blocks_gone():
+        for i in range(4):
+            for j in range(4):
+                if j:
+                    onward(i, j).wait_send()
+                to_sibling(i, j).wait_send()
+
+    pending.append(blocks_gone)
+    take_blocks(False)
 
     def lane_sums(values):
         part = values[:, 0:128] + values[:, 128:256] + values[:, 256:384]
@@ -290,6 +334,7 @@
     has_right = jnp.where(s < FRAMES - 1, 1.0, 0.0)
     rim_up.wait_recv()
     rim_down.wait_recv()
+    take_blocks(True)
     wtime = wbuf[:, TIME_AT:COLS]
     taps = [wtime[:, k * CH : (k + 1) * CH] for k in range(3)]
     grads = (ogr[1], og_ref[...], ogr[0])
@@ -367,14 +412,6 @@
 
     scaled = act_grad * (sig * (1.0 + preact * (1.0 - sig))) * gain
     exchange(st2, sums_of(scaled, scaled * normed), st2_s, st2_r)
-    arim_up = copy(act_ref, actr.at[0], arim_s.at[0], arim_r.at[0], f, (s + 1) % 16)
-    arim_down = copy(act_ref, actr.at[1], arim_s.at[1], arim_r.at[1], f, (s + 15) % 16)
-    start(arim_up)
-    start(arim_down)
-
-    arrived(st2, st2_s, st2_r)
-    mean_one, mean_two = group_means(st2)
-    hid_grad = (inv_std * (scaled - mean_one - normed * mean_two)).astype(BF16)
 
     def gp_take(j):
         src = (chip - j + 16) % 16
@@ -401,6 +438,15 @@
 
     loop(0, 31, lambda i: to_owner(flight_order(i), lambda cp: cp.start()))
     pending.append(lambda: loop(1, 32, lambda d: to_owner(d, lambda cp: cp.wait_send())))
+
+    arim_up = copy(act_ref, actr.at[0], arim_s.at[0], arim_r.at[0], f, (s + 1) % 16)
+    arim_down = copy(act_ref, actr.at[1], arim_s.at[1], arim_r.at[1], f, (s + 15) % 16)
+    start(arim_up)
+    start(arim_down)
+
+    arrived(st2, st2_s, st2_r)
+    mean_one, mean_two = group_means(st2)
+    hid_grad = (inv_std * (scaled - mean_one - normed * mean_two)).astype(BF16)
 
     wtrans[...] = wbuf[:, 0:TIME_AT].T
     total = nn(wtrans[4 * CH : 5 * CH, :], hid_grad)
@@ -421,6 +467,9 @@
     mixed_out = pltpu.make_async_copy(mixed_ref, mixed_hbm, out_sem.at[1])
     mixed_out.start()
 
+    for left_over in pending:
+        left_over()
+
     def fin_copy(j, src):
         return copy(fval, fin.at[src], fin_s.at[j], fin_r.at[src], f, (s + j) % 16)
 
@@ -447,41 +496,30 @@
     def _():
         loop(1, 16, lambda j: fin_copy(j, chip % 8).wait_send())
 
-    for left_over in pending:
-        left_over()
     ing_out.wait()
     mixed_out.wait()
     gt_out.wait()
 
 
-def hand_over(mixed_in, ing_in, gt_in, mixed_out, ing_out, gt_out, sems):
-    copies = [
-        pltpu.make_async_copy(src, dst, sems.at[n])
-        for n, (src, dst) in enumerate(((mixed_in, mixed_out), (ing_in, ing_out), (gt_in, gt_out)))
-    ]
-    for cp in copies:
-        cp.start()
-    for cp in copies:
-        cp.wait()
-
-
 def local(clips_in, weight_space, weight_time, norm_gain, norm_shift, out_grad):
-    vmem = pl.BlockSpec(memory_space=pltpu.VMEM)
     dma = pltpu.SemaphoreType.DMA
-    hbm = pl.BlockSpec(memory_space=pl.ANY)
-    results = pl.pallas_call(
+    hbm = pl.BlockSpec(memory_space=pltpu.HBM)
+    anywhere = pl.BlockSpec(memory_space=pl.ANY)
+    mixed, in_grad, grad_time = pl.pallas_call(
         kernel,
         out_shape=(
             jax.ShapeDtypeStruct((CH, PIXELS), BF16),
             jax.ShapeDtypeStruct((CH, PIXELS), BF16),
             jax.ShapeDtypeStruct((5, 3 * CH), F32),
         ),
-        in_specs=[hbm, hbm, hbm, vmem, vmem, hbm],
-        out_specs=(hbm, hbm, hbm),
+        in_specs=[hbm] * 6,
+        out_specs=(anywhere, anywhere, anywhere),
         scratch_shapes=[
             pltpu.VMEM((CH, PIXELS), BF16),
             pltpu.VMEM((5, 9 * CH), BF16),
             pltpu.VMEM((5, 3 * CH), BF16),
+            pltpu.VMEM((CH,), F32),
+            pltpu.VMEM((CH,), F32),
             pltpu.VMEM((CH, PIXELS), BF16),
             pltpu.VMEM((CH, PIXELS), BF16),
             pltpu.VMEM((CH, PIXELS), BF16),
@@ -511,25 +549,23 @@
         + [dma((1,))] * 2
         + [dma((16,))] * 2
         + [dma((NZ,))] * 2
-        + [dma((16,)), dma((8,)), dma((4,)), dma((3,))],
+        + [dma((16,)), dma((8,)), dma((6,)), dma((3,))],
         compiler_params=pltpu.CompilerParams(
-            collective_id=0, has_side_effects=True, vmem_limit_bytes=56 * 1024 * 1024
+            collective_id=0, has_side_effects=True, vmem_limit_bytes=24 * 1024 * 1024
         ),
     )(
-        clips_in.reshape(PIXELS, CH).T,
-        weight_space,
-        weight_time,
-        norm_gain,
-        norm_shift,
-        out_grad.reshape(PIXELS, CH).T,
+        *(
+            pltpu.with_memory_space_constraint(v, pltpu.HBM)
+            for v in (
+                clips_in.reshape(PIXELS, CH).T,
+                weight_space,
+                weight_time,
+                norm_gain,
+                norm_shift,
+                out_grad.reshape(PIXELS, CH).T,
+            )
+        )
     )
-    mixed, in_grad, grad_time = pl.pallas_call(
-        hand_over,
-        out_shape=tuple(jax.ShapeDtypeStruct(v.shape, v.dtype) for v in results),
-        in_specs=[hbm] * 3,
-        out_specs=(hbm,) * 3,
-        scratch_shapes=[dma((3,))],
-    )(*results)
     return mixed.T.reshape(clips_in.shape), in_grad.T.reshape(clips_in.shape), grad_time
 
 

time: 118 us -> 97.3 us (0.82)
  Pallas kernels: 117 us -> 94.5 us
  local copies, waits for them, and re-layouts: 0 us -> 2 us
    pallas_call x1 -> x0, Pallas kernels: 17 us -> none  [local(): pl.pallas_call(hand_over, out_shape=tuple((jax.ShapeDtypeStruct(v.shape,...]
    pallas_call x1, Pallas kernels: 100 us -> 94.5 us  [local(): pl.pallas_call(kernel, out_shape=(jax.ShapeDtypeStruct((CH, PIXELS), BF16...]
    unnamed x0 -> x3, local copies, waits for them, and re-layouts: none -> 2 us
where the time goes in v4:
time: 97.3 us; the launch traced here: 97.2 us
  Pallas kernels  94.5 us (97%)
  local copies, waits for them, and re-layouts  2 us (2%)
    pallas_call x1, Pallas kernels, local(): pl.pallas_call(kernel, out_shape=(jax.ShapeDtypeStruct((CH, PIXELS), BF16...  94.5 us
    unnamed x3, local copies, waits for them, and re-layouts  2 us

profile of v4, /device:TPU:1, one launch (start us, length us, event | category | flops | bytes accessed | tf_op | source)
XLA Modules:
  0.0 97.2 jit_solution(9453124809236931892)
XLA Ops:
  0.6 94.5 %shard_map.85 = (bf16[320,384]{1,0:T(8,128)(2,1)S(1)}, bf16[320,384]{1,0:T(8,128)(2,1)S(1)}, f32[5,960]{1,0:T(8,128)S(1)}) custom-call(bf16[320,384]{1,0:T(8,128)(2,1)} %bitcast.14, bf16[5,2880]{1,0:T(8,128)(2,1)} %ws_hbm.1, bf16[5,960]{1,0:T(8,128)(2,1)} %wt_hbm.1, f32[320]{0:T(512)} %gain_hbm.1, f32[320]{0:T(512)} %shift_hbm.1, bf16[320,384]{1,0:T(8,128)(2,1)} %bitcast.15), custom_call_target="tpu_custom_call" | custom-call | tf_op jit(solution)/shard_map/pallas_call | solution.py:508
  95.2 0.7 copy.12
  95.9 0.7 copy.13
  96.6 0.6 copy.14

commit v5 on v4

--- a/solution.py
+++ b/solution.py
@@ -269,8 +269,6 @@
             ref = wblock(*first_block(i), c)
             copy(ref, ref, p1_s.at[i], p1_r.at[i], f, sib).wait_recv()
         pl.when(first_block(i)[1] < 3)(lambda i=i: forward(i))
-    for i in range(4):
-        pl.when(first_block(i)[1] == 3)(lambda i=i: forward(i))
 
     def second(i, j):
         ref = wblock(*second_block(i, j, c), c)
@@ -283,16 +281,18 @@
         n = 4 * j + i
         copy(ref, ref, p3_s.at[n], p3_r.at[n], f, sib).wait_recv()
 
-    def take_blocks(temporal):
-        def wanted(bx):
-            return bx == 3 if temporal else bx < 3
-
+    def wanted(bx, temporal):
+        return bx == 3 if temporal else bx < 3
+
+    def take_own(temporal):
         for i in range(4):
             for j in range(1, 4):
-                pl.when(wanted(second_block(i, j, c)[1]))(lambda i=i, j=j: second(i, j))
+                pl.when(wanted(second_block(i, j, c)[1], temporal))(lambda i=i, j=j: second(i, j))
+
+    def take_sibling(temporal):
         for i in range(4):
             for j in range(4):
-                pl.when(wanted(second_block(i, j, 1 - c)[1]))(lambda i=i, j=j: from_sibling(i, j))
+                pl.when(wanted(second_block(i, j, 1 - c)[1], temporal))(lambda i=i, j=j: from_sibling(i, j))
 
     def blocks_gone():
         for i in range(4):
@@ -302,7 +302,9 @@
                 to_sibling(i, j).wait_send()
 
     pending.append(blocks_gone)
-    take_blocks(False)
+    take_own(False)
+    for i in range(4):
+        pl.when(first_block(i)[1] == 3)(lambda i=i: forward(i))
 
     def lane_sums(values):
         part = values[:, 0:128] + values[:, 128:256] + values[:, 256:384]
@@ -327,26 +329,20 @@
 
         loop(1, 16, take)
 
-    hidden = nn(wbuf[:, 0:TIME_AT], xcol[...])
+    def columns_of(cc):
+        cols = pl.ds(pl.multiple_of(cc * (TIME_AT // 2), BLK), TIME_AT // 2)
+        return nn(wbuf[:, cols], xcol[cols, :])
+
+    hidden = columns_of(c)
+    take_sibling(False)
+    hidden = hidden + columns_of(1 - c)
     exchange(st1, sums_of(hidden, hidden * hidden), st1_s, st1_r)
+    wtrans[...] = wbuf[:, 0:TIME_AT].T
 
     has_left = jnp.where(s > 0, 1.0, 0.0)
     has_right = jnp.where(s < FRAMES - 1, 1.0, 0.0)
     rim_up.wait_recv()
     rim_down.wait_recv()
-    take_blocks(True)
-    wtime = wbuf[:, TIME_AT:COLS]
-    taps = [wtime[:, k * CH : (k + 1) * CH] for k in range(3)]
-    grads = (ogr[1], og_ref[...], ogr[0])
-    act_grad = (
-        (
-            nn(taps[0].T, grads[0]) * has_right
-            + nn(taps[1].T, grads[1])
-            + nn(taps[2].T, grads[2]) * has_left
-        )
-        .astype(BF16)
-        .astype(F32)
-    )
     per = CH // GROUPS
     row_i = lax.broadcasted_iota(jnp.int32, (CH, CH), 0)
     col_i = lax.broadcasted_iota(jnp.int32, (CH, CH), 1)
@@ -402,19 +398,36 @@
     def tile_of(q):
         return gchip.at[q // 8, :, pl.ds(pl.multiple_of((q % 8) * 128, 128), 128)]
 
+    def plane_step(j):
+        return ((y + j // 4) % 4) * 4 + (x + j % 4) % 4
+
     def gp_copy(j, to, src):
         fd, sd = on_chip(to, c)
         return copy(tile_of(to), gplane.at[src], gp_s.at[j], gp_r.at[j], fd, sd)
 
-    loop(1, 16, lambda j: gp_copy(j, (chip + j) % 16, chip).start())
-    pending.append(lambda: loop(1, 16, lambda j: gp_copy(j, (chip + j) % 16, chip).wait_send()))
+    for j in sorted(range(1, 16), key=lambda j: -min(j // 4, 4 - j // 4) - min(j % 4, 4 - j % 4)):
+        gp_copy(j, plane_step(j), chip).start()
+    pending.append(lambda: loop(1, 16, lambda j: gp_copy(j, plane_step(j), chip).wait_send()))
     gplane[chip] = gchip[chip // 8, :, pl.ds(pl.multiple_of((chip % 8) * 128, 128), 128)]
 
+    take_own(True)
+    take_sibling(True)
+    wtime = wbuf[:, TIME_AT:COLS]
+    taps = [wtime[:, k * CH : (k + 1) * CH] for k in range(3)]
+    act_grad = (
+        (
+            nn(taps[0].T, ogr[1]) * has_right
+            + nn(taps[1].T, og_ref[...])
+            + nn(taps[2].T, ogr[0]) * has_left
+        )
+        .astype(BF16)
+        .astype(F32)
+    )
     scaled = act_grad * (sig * (1.0 + preact * (1.0 - sig))) * gain
     exchange(st2, sums_of(scaled, scaled * normed), st2_s, st2_r)
 
     def gp_take(j):
-        src = (chip - j + 16) % 16
+        src = plane_step(16 + 4 * ((4 - j // 4) % 4) + (4 - j % 4) % 4)
         gp_copy(j, src, src).wait_recv()
 
     loop(1, 16, gp_take)
@@ -448,7 +461,6 @@
     mean_one, mean_two = group_means(st2)
     hid_grad = (inv_std * (scaled - mean_one - normed * mean_two)).astype(BF16)
 
-    wtrans[...] = wbuf[:, 0:TIME_AT].T
     total = nn(wtrans[4 * CH : 5 * CH, :], hid_grad)
     for a in range(3):
         for b in range(3):

time: 97.3 us -> 96.9 us (level)
  no operation moved by 1% of the time
where the time goes in v5:
time: 96.9 us; the launch traced here: 96.8 us
  Pallas kernels  94.1 us (97%)
  local copies, waits for them, and re-layouts  2 us (2%)
    pallas_call x1, Pallas kernels, local(): pl.pallas_call(kernel, out_shape=(jax.ShapeDtypeStruct((CH, PIXELS), BF16...  94.1 us
    unnamed x3, local copies, waits for them, and re-layouts  2 us

profile of v5, /device:TPU:1, one launch (start us, length us, event | category | flops | bytes accessed | tf_op | source)
XLA Modules:
  0.0 96.8 jit_solution(7603673083936797323)
XLA Ops:
  0.6 94.1 %shard_map.85 = (bf16[320,384]{1,0:T(8,128)(2,1)S(1)}, bf16[320,384]{1,0:T(8,128)(2,1)S(1)}, f32[5,960]{1,0:T(8,128)S(1)}) custom-call(bf16[320,384]{1,0:T(8,128)(2,1)} %bitcast.14, bf16[5,2880]{1,0:T(8,128)(2,1)} %ws_hbm.1, bf16[5,960]{1,0:T(8,128)(2,1)} %wt_hbm.1, f32[320]{0:T(512)} %gain_hbm.1, f32[320]{0:T(512)} %shift_hbm.1, bf16[320,384]{1,0:T(8,128)(2,1)} %bitcast.15), custom_call_target="tpu_custom_call" | custom-call | tf_op jit(solution)/shard_map/pallas_call | solution.py:520
  94.8 0.7 copy.12
  95.5 0.7 copy.13
  96.2 0.6 copy.14
